TPU v7x, 256 devices: a whole 4x4x8 slice. The times are simulated.
256 devices in a mesh: blk: 64 (over y_lo, z, x), rep: 4 (over y_hi, core).
Axes of the slice: x: 4, y: 4 (y_hi: 2, y_lo: 2; y = y_hi * 2 + y_lo), z: 8, core: 2. Of those that a mesh axis runs over, the one named last changes fastest.
Arguments:
- points: bfloat16 [49152, 1024], P('blk'), may hold values from -6 to 6
- w_in: bfloat16 [1024, 512], replicated, may hold values from -0.1875 to 0.1875
- b_in: float32 [512], replicated, may hold values from -3 to 3
- w_out: bfloat16 [512, 64], replicated, may hold values from -0.25 to 0.25
- inv_scale: float32 [64], replicated, may hold values from 0.05 to 0.5
- solves: bfloat16 [64, 49152], P(None, 'blk'), may hold values from -1 to 1
- probes: bfloat16 [64, 49152], P(None, 'blk'), may hold values from -1 to 1
Outputs:
- feat_grad: float32 [64, 49152], P(None, ('blk', 'rep'))
- grad_w_in: float32 [1024, 512], replicated
- grad_b_in: float32 [512], replicated
- grad_w_out: float32 [512, 64], replicated
All inputs are finite; a program needn't handle non-finite values.
Results may differ from a plain program's by a relative error of at most 0.034.
Values may be sent and summed in bfloat16 or wider, within the bound.
A program may use at most 64 MiB of HBM per device.

v0:
```python
import math

import jax
import jax.numpy as jnp
from jax import lax
from jax.sharding import PartitionSpec as P


def shifted(block, axis, distance):
    devices = range(lax.axis_size(axis))
    route = [((i - distance) % len(devices), i) for i in devices]
    return lax.ppermute(block, axis, route)


def cut_along(value, dim, count):
    lengths = value.shape
    blocks = value.reshape(*lengths[:dim], count, lengths[dim] // count, *lengths[dim + 1 :])
    return jnp.moveaxis(blocks, dim, 0)


def sum_at_owner(value, axis, dim):
    count = lax.axis_size(axis)
    blocks = lax.all_to_all(cut_along(value, dim, count), axis, 0, 0, tiled=True)
    return jnp.sum(blocks, axis=0)


def couple(own_y, own_pair, own_sq, visitor, feat):
    vis_y = visitor[:feat]
    vis_pair = visitor[feat:]
    vis_sq = jnp.sum(jnp.square(vis_y.astype(jnp.float32)), axis=0)
    cross = lax.dot_general(
        own_y, vis_y, (((0,), (0,)), ((), ())), preferred_element_type=jnp.float32
    )
    kernel = jnp.exp(-0.5 * (own_sq[:, None] + vis_sq[None, :] - 2.0 * cross))
    coupling = lax.dot_general(
        own_pair, vis_pair, (((0,), (0,)), ((), ())), preferred_element_type=jnp.float32
    )
    weight_b = (coupling * kernel).astype(jnp.bfloat16)
    totals = jnp.sum(weight_b.astype(jnp.float32), axis=1)
    pull = lax.dot_general(
        vis_y, weight_b, (((1,), (1,)), ((), ())), preferred_element_type=jnp.float32
    )
    return (totals, pull)


def on_device(points, w_in, b_in, w_out, inv_scale, solves, probes):
    feat = w_out.shape[1]
    reps = lax.axis_size("rep")
    blocks = lax.axis_size("blk")
    rep_index = lax.axis_index("rep")
    rows = points.shape[0]
    quarter = rows // reps
    first = rep_index * quarter
    npts = rows * blocks
    levels = reps.bit_length() - 1
    own_points = lax.dynamic_slice_in_dim(points, first, quarter, 0)
    hidden = jnp.tanh(jnp.dot(points, w_in, preferred_element_type=jnp.float32) + b_in).astype(
        jnp.bfloat16
    )
    pre = lax.dot_general(
        w_out, hidden, (((0,), (1,)), ((), ())), preferred_element_type=jnp.float32
    )
    hidden, scaled = (hidden, (pre * inv_scale[:, None]).astype(jnp.bfloat16))
    own_hidden = lax.dynamic_slice_in_dim(hidden, first, quarter, 0)
    own_pair = jnp.concatenate([solves, probes], axis=0)
    own_sq = jnp.sum(jnp.square(scaled.astype(jnp.float32)), axis=0)
    scaled32 = scaled.astype(jnp.float32)
    visitor = jnp.concatenate([scaled, probes, solves], axis=0)
    for bit in range(levels):
        moved = shifted(visitor, "blk", -(1 << bit))
        visitor = jnp.where(rep_index // (1 << bit) % 2 == 1, moved, visitor)

    def accumulate(state, vis):
        totals, pull = couple(scaled, own_pair, own_sq, vis, feat)
        return (state[0] + totals, state[1] + pull)

    init = (jnp.zeros((rows,), jnp.float32), jnp.zeros((feat, rows), jnp.float32))
    steps = blocks // reps
    behind = shifted(visitor, "blk", reps)

    def advance_both(index, carry):
        state, ahead_vis, behind_vis = carry
        state = accumulate(accumulate(state, ahead_vis), behind_vis)
        ahead_vis = shifted(ahead_vis, "blk", -reps)
        behind_vis = shifted(behind_vis, "blk", reps)
        return (state, ahead_vis, behind_vis)

    state, ahead_vis, behind_vis = lax.fori_loop(
        0, steps // 2 - 1, advance_both, (init, visitor, behind)
    )
    state = accumulate(accumulate(state, ahead_vis), behind_vis)
    totals, pull = state
    drift = pull - scaled32 * totals[None, :]
    summed = sum_at_owner(drift, "rep", 1)
    feat_grad = summed * inv_scale[:, None]
    grad_b16 = feat_grad.astype(jnp.bfloat16)
    back = lax.dot_general(
        grad_b16, w_out, (((0,), (1,)), ((), ())), preferred_element_type=jnp.float32
    )
    hid32 = own_hidden.astype(jnp.float32)
    pre_grad = back * (1.0 - hid32 * hid32)
    norm = 1.0 / math.sqrt(npts)
    term_w_in = (
        lax.dot_general(
            own_points,
            pre_grad.astype(jnp.bfloat16),
            (((0,), (0,)), ((), ())),
            preferred_element_type=jnp.float32,
        )
        * norm
    )
    term_b_in = jnp.sum(pre_grad, axis=0) * norm
    term_w_out = (
        lax.dot_general(
            own_hidden, grad_b16, (((0,), (1,)), ((), ())), preferred_element_type=jnp.float32
        )
        * norm
    )
    grad_w_in, grad_b_in, grad_w_out = lax.psum((term_w_in, term_b_in, term_w_out), ("blk", "rep"))
    return (feat_grad, grad_w_in, grad_b_in, grad_w_out)


def solution(mesh):
    in_specs = (P("blk", None), P(), P(), P(), P(), P(None, "blk"), P(None, "blk"))
    out_specs = (P(None, ("blk", "rep")), P(), P(), P())
    return jax.shard_map(
        on_device, mesh=mesh, in_specs=in_specs, out_specs=out_specs, check_vma=False
    )
```

profile of v0, /device:TPU:1, one launch (start us, length us, event | category | flops | bytes accessed | tf_op | source)
XLA Modules:
  0.0 442.3 jit_solution(13951835075255544906)
XLA Ops:
  8.6 2.2 tanh_convert_fusion
  13.6 9.7 %collective-permute-start.2 = (bf16[192,768]{1,0:T(8,128)(2,1)S(1)}, bf16[192,768]{1,0:T(8,128)(2,1)S(1)}, u32[]{:S(2)}, u32[]{:S(2)}) collective-permute-start(bf16[192,768]{1,0:T(8,128)(2,1)S(1)} %pad_maximum_fusion), channel_id=1, source_target_pairs={{4,0},{8,4},{12,8},{16,12},{20,16},{24,20},{28,24},{32,28},{36,32}... | collective-permute-start | bytes 884744 | tf_op jit(solution)/shard_map/ppermute | solution.py:12
  23.3 5.7 %collective-permute-done.2 = bf16[192,768]{1,0:T(8,128)(2,1)S(1)} collective-permute-done((bf16[192,768]{1,0:T(8,128)(2,1)S(1)}, bf16[192,768]{1,0:T(8,128)(2,1)S(1)}, u32[]{:S(2)}, u32[]{:S(2)}) %collective-permute-start.2) | collective-permute-done | bytes 294944 | tf_op jit(solution)/shard_map/ppermute | solution.py:12
  30.0 2.5 collective-permute-start.3
  32.5 6.0 %collective-permute-done.3 = bf16[192,768]{1,0:T(8,128)(2,1)S(1)} collective-permute-done((bf16[192,768]{1,0:T(8,128)(2,1)S(1)}, bf16[192,768]{1,0:T(8,128)(2,1)S(1)}, u32[]{:S(2)}, u32[]{:S(2)}) %collective-permute-start.3) | collective-permute-done | bytes 294944 | tf_op jit(solution)/shard_map/ppermute | solution.py:12
  39.3 8.4 %collective-permute-done.4 = bf16[192,768]{1,0:T(8,128)(2,1)} collective-permute-done((bf16[192,768]{1,0:T(8,128)(2,1)}, bf16[192,768]{1,0:T(8,128)(2,1)}, u32[]{:S(2)}, u32[]{:S(2)}) %collective-permute-start.4) | collective-permute-done | bytes 294944 | tf_op jit(solution)/shard_map/ppermute | solution.py:12
  47.7 89.4 %while.17 = (s32[]{:T(128)}, f32[768]{0:T(1024)S(1)}, f32[64,768]{1,0:T(8,128)}, bf16[192,768]{1,0:T(8,128)(2,1)}, bf16[192,768]{1,0:T(8,128)(2,1)}, /*index=5*/...) while((s32[]{:T(128)}, f32[768]{0:T(1024)S(1)}, ...), condition=%wide.region_6.7_spmd.clone, body=%wide.region_1.6_spmd.clone.sunk | while | flops 613858560 | bytes 20095168 | solution.py:88
  59.7 2.1 collective-permute-start
  68.5 2.0 fusion.79
  71.5 3.6 collective-permute-start
  81.8 2.0 fusion.79
  84.8 3.6 collective-permute-start
  95.1 2.0 fusion.79
  98.1 3.6 collective-permute-start
  108.4 2.0 fusion.79
  111.4 3.6 collective-permute-start
  121.7 2.0 fusion.79
  124.7 3.6 collective-permute-start
  135.0 2.0 fusion.79
  148.3 12.0 %all-to-all-start = ((f32[4,64,192]{2,1,0:T(8,128)}), f32[4,64,192]{2,1,0:T(8,128)S(1)}, u32[]{:S(2)}, u32[]{:S(2)}) async-start(f32[4,64,192]{2,1,0:T(8,128)} %bitcast.31), calls=%async_computation | async-start | bytes 524288 | tf_op jit(solution)/shard_map/all_to_all | solution.py:23
  160.3 6.7 %all-to-all-done = f32[4,64,192]{2,1,0:T(8,128)S(1)} async-done(((f32[4,64,192]{2,1,0:T(8,128)}), f32[4,64,192]{2,1,0:T(8,128)S(1)}, u32[]{:S(2)}, u32[]{:S(2)}) %all-to-all-start) | async-done | bytes 196640 | tf_op jit(solution)/shard_map/all_to_all | solution.py:23
  170.0 81.2 %psum.22 = f32[512]{0:T(512)} all-reduce(f32[512]{0:T(512)S(1)} %broadcast_multiply_fusion.1), channel_id=1, replica_groups=mesh['blk'=64,'rep'=4] {'blk','rep'}, use_global_device_ids=true, to_apply=%region_14.15 | all-reduce | flops 512 | bytes 4096 | tf_op jit(solution)/shard_map/psum | solution.py:119
  251.3 180.4 %all-reduce.3.cloned.1.call-done = (f32[1024,512]{1,0:T(8,128)}, f32[512,64]{0,1:T(8,128)}) async-done(((f32[1024,512]{1,0:T(8,128)}, f32[512,64]{0,1:T(8,128)}), (f32[1024,512]{1,0:T(8,128)}, f32[512,64]{0,1:T(8,128)})) %all-reduce.3.cloned.1.call-update) | async-done | bytes 2228240 | tf_op jit(solution)/shard_map/psum | solution.py:119
  431.7 3.1 copy.32
  (138 shorter events, 77.5 us)
Async XLA Ops:
  7.2 4.5 %copy-start.8 = (bf16[512,64]{0,1:T(8,128)(2,1)S(1)}, bf16[512,64]{0,1:T(8,128)(2,1)}, u32[]{:S(2)}) copy-start(bf16[512,64]{0,1:T(8,128)(2,1)} %param.12) | copy-start | bytes 196612
  7.2 5.5 %copy-start.4 = (bf16[64,768]{1,0:T(8,128)(2,1)S(1)}, bf16[64,768]{1,0:T(8,128)(2,1)}, u32[]{:S(2)}) copy-start(bf16[64,768]{1,0:T(8,128)(2,1)} %param.14) | copy-start | bytes 294916
  13.6 15.4 %collective-permute-start.2 = (bf16[192,768]{1,0:T(8,128)(2,1)S(1)}, bf16[192,768]{1,0:T(8,128)(2,1)S(1)}, u32[]{:S(2)}, u32[]{:S(2)}) collective-permute-start(bf16[192,768]{1,0:T(8,128)(2,1)S(1)} %pad_maximum_fusion), channel_id=1, source_target_pairs={{4,0},{8,4},{12,8},{16,12},{20,16},{24,20},{28,24},{32,28},{36,32}... | collective-permute-start | bytes 884744 | tf_op jit(solution)/shard_map/ppermute | solution.py:12
  30.0 8.5 %collective-permute-start.3 = (bf16[192,768]{1,0:T(8,128)(2,1)S(1)}, bf16[192,768]{1,0:T(8,128)(2,1)S(1)}, u32[]{:S(2)}, u32[]{:S(2)}) collective-permute-start(bf16[192,768]{1,0:T(8,128)(2,1)S(1)} %broadcast_select_fusion), channel_id=1, source_target_pairs={{8,0},{12,4},{16,8},{20,12},{24,16},{28,20},{32,24},{36,28},{40,32... | collective-permute-start | bytes 884744 | tf_op jit(solution)/shard_map/ppermute | solution.py:12
  39.2 8.4 %collective-permute-start.4 = (bf16[192,768]{1,0:T(8,128)(2,1)}, bf16[192,768]{1,0:T(8,128)(2,1)}, u32[]{:S(2)}, u32[]{:S(2)}) collective-permute-start(bf16[192,768]{1,0:T(8,128)(2,1)} %broadcast_select_fusion.1), channel_id=1, source_target_pairs={{240,0},{244,4},{248,8},{252,12},{0,16},{4,20},{8,24},{12,28},{16,... | collective-permute-start | bytes 884744 | tf_op jit(solution)/shard_map/ppermute | solution.py:12
  48.6 10.1 %collective-permute-start = (bf16[192,768]{1,0:T(8,128)(2,1)S(1)}, bf16[192,768]{1,0:T(8,128)(2,1)}, u32[]{:S(2)}, u32[]{:S(2)}) collective-permute-start(bf16[192,768]{1,0:T(8,128)(2,1)S(1)} %copy.23), channel_id=1, source_target_pairs={{16,0},{20,4},{24,8},{28,12},{32,16},{36,20},{40,24},{44,28},{48,3... | collective-permute-start | bytes 884744 | tf_op jit(solution)/shard_map/while/body/eval_jaxpr/ppermute | solution.py:12
  49.6 9.2 %collective-permute-start.1 = (bf16[192,768]{1,0:T(8,128)(2,1)S(1)}, bf16[192,768]{1,0:T(8,128)(2,1)}, u32[]{:S(2)}, u32[]{:S(2)}) collective-permute-start(bf16[192,768]{1,0:T(8,128)(2,1)S(1)} %copy.24), channel_id=1, source_target_pairs={{240,0},{244,4},{248,8},{252,12},{0,16},{4,20},{8,24},{12,28},{16,... | collective-permute-start | bytes 884744 | tf_op jit(solution)/shard_map/while/body/eval_jaxpr/ppermute | solution.py:12
  59.7 10.8 %collective-permute-start = (bf16[192,768]{1,0:T(8,128)(2,1)S(1)}, bf16[192,768]{1,0:T(8,128)(2,1)}, u32[]{:S(2)}, u32[]{:S(2)}) collective-permute-start(bf16[192,768]{1,0:T(8,128)(2,1)S(1)} %copy.23), channel_id=1, source_target_pairs={{16,0},{20,4},{24,8},{28,12},{32,16},{36,20},{40,24},{44,28},{48,3... | collective-permute-start | bytes 884744 | tf_op jit(solution)/shard_map/while/body/eval_jaxpr/ppermute | solution.py:12
  62.8 7.8 %collective-permute-start.1 = (bf16[192,768]{1,0:T(8,128)(2,1)S(1)}, bf16[192,768]{1,0:T(8,128)(2,1)}, u32[]{:S(2)}, u32[]{:S(2)}) collective-permute-start(bf16[192,768]{1,0:T(8,128)(2,1)S(1)} %copy.24), channel_id=1, source_target_pairs={{240,0},{244,4},{248,8},{252,12},{0,16},{4,20},{8,24},{12,28},{16,... | collective-permute-start | bytes 884744 | tf_op jit(solution)/shard_map/while/body/eval_jaxpr/ppermute | solution.py:12
  71.5 12.3 %collective-permute-start = (bf16[192,768]{1,0:T(8,128)(2,1)S(1)}, bf16[192,768]{1,0:T(8,128)(2,1)}, u32[]{:S(2)}, u32[]{:S(2)}) collective-permute-start(bf16[192,768]{1,0:T(8,128)(2,1)S(1)} %copy.23), channel_id=1, source_target_pairs={{16,0},{20,4},{24,8},{28,12},{32,16},{36,20},{40,24},{44,28},{48,3... | collective-permute-start | bytes 884744 | tf_op jit(solution)/shard_map/while/body/eval_jaxpr/ppermute | solution.py:12
  76.1 7.8 %collective-permute-start.1 = (bf16[192,768]{1,0:T(8,128)(2,1)S(1)}, bf16[192,768]{1,0:T(8,128)(2,1)}, u32[]{:S(2)}, u32[]{:S(2)}) collective-permute-start(bf16[192,768]{1,0:T(8,128)(2,1)S(1)} %copy.24), channel_id=1, source_target_pairs={{240,0},{244,4},{248,8},{252,12},{0,16},{4,20},{8,24},{12,28},{16,... | collective-permute-start | bytes 884744 | tf_op jit(solution)/shard_map/while/body/eval_jaxpr/ppermute | solution.py:12
  84.8 12.3 %collective-permute-start = (bf16[192,768]{1,0:T(8,128)(2,1)S(1)}, bf16[192,768]{1,0:T(8,128)(2,1)}, u32[]{:S(2)}, u32[]{:S(2)}) collective-permute-start(bf16[192,768]{1,0:T(8,128)(2,1)S(1)} %copy.23), channel_id=1, source_target_pairs={{16,0},{20,4},{24,8},{28,12},{32,16},{36,20},{40,24},{44,28},{48,3... | collective-permute-start | bytes 884744 | tf_op jit(solution)/shard_map/while/body/eval_jaxpr/ppermute | solution.py:12
  89.4 7.8 %collective-permute-start.1 = (bf16[192,768]{1,0:T(8,128)(2,1)S(1)}, bf16[192,768]{1,0:T(8,128)(2,1)}, u32[]{:S(2)}, u32[]{:S(2)}) collective-permute-start(bf16[192,768]{1,0:T(8,128)(2,1)S(1)} %copy.24), channel_id=1, source_target_pairs={{240,0},{244,4},{248,8},{252,12},{0,16},{4,20},{8,24},{12,28},{16,... | collective-permute-start | bytes 884744 | tf_op jit(solution)/shard_map/while/body/eval_jaxpr/ppermute | solution.py:12
  98.1 12.3 %collective-permute-start = (bf16[192,768]{1,0:T(8,128)(2,1)S(1)}, bf16[192,768]{1,0:T(8,128)(2,1)}, u32[]{:S(2)}, u32[]{:S(2)}) collective-permute-start(bf16[192,768]{1,0:T(8,128)(2,1)S(1)} %copy.23), channel_id=1, source_target_pairs={{16,0},{20,4},{24,8},{28,12},{32,16},{36,20},{40,24},{44,28},{48,3... | collective-permute-start | bytes 884744 | tf_op jit(solution)/shard_map/while/body/eval_jaxpr/ppermute | solution.py:12
  102.7 7.8 %collective-permute-start.1 = (bf16[192,768]{1,0:T(8,128)(2,1)S(1)}, bf16[192,768]{1,0:T(8,128)(2,1)}, u32[]{:S(2)}, u32[]{:S(2)}) collective-permute-start(bf16[192,768]{1,0:T(8,128)(2,1)S(1)} %copy.24), channel_id=1, source_target_pairs={{240,0},{244,4},{248,8},{252,12},{0,16},{4,20},{8,24},{12,28},{16,... | collective-permute-start | bytes 884744 | tf_op jit(solution)/shard_map/while/body/eval_jaxpr/ppermute | solution.py:12
  111.4 12.3 %collective-permute-start = (bf16[192,768]{1,0:T(8,128)(2,1)S(1)}, bf16[192,768]{1,0:T(8,128)(2,1)}, u32[]{:S(2)}, u32[]{:S(2)}) collective-permute-start(bf16[192,768]{1,0:T(8,128)(2,1)S(1)} %copy.23), channel_id=1, source_target_pairs={{16,0},{20,4},{24,8},{28,12},{32,16},{36,20},{40,24},{44,28},{48,3... | collective-permute-start | bytes 884744 | tf_op jit(solution)/shard_map/while/body/eval_jaxpr/ppermute | solution.py:12
  116.0 7.8 %collective-permute-start.1 = (bf16[192,768]{1,0:T(8,128)(2,1)S(1)}, bf16[192,768]{1,0:T(8,128)(2,1)}, u32[]{:S(2)}, u32[]{:S(2)}) collective-permute-start(bf16[192,768]{1,0:T(8,128)(2,1)S(1)} %copy.24), channel_id=1, source_target_pairs={{240,0},{244,4},{248,8},{252,12},{0,16},{4,20},{8,24},{12,28},{16,... | collective-permute-start | bytes 884744 | tf_op jit(solution)/shard_map/while/body/eval_jaxpr/ppermute | solution.py:12
  124.7 12.3 %collective-permute-start = (bf16[192,768]{1,0:T(8,128)(2,1)S(1)}, bf16[192,768]{1,0:T(8,128)(2,1)}, u32[]{:S(2)}, u32[]{:S(2)}) collective-permute-start(bf16[192,768]{1,0:T(8,128)(2,1)S(1)} %copy.23), channel_id=1, source_target_pairs={{16,0},{20,4},{24,8},{28,12},{32,16},{36,20},{40,24},{44,28},{48,3... | collective-permute-start | bytes 884744 | tf_op jit(solution)/shard_map/while/body/eval_jaxpr/ppermute | solution.py:12
  129.3 7.8 %collective-permute-start.1 = (bf16[192,768]{1,0:T(8,128)(2,1)S(1)}, bf16[192,768]{1,0:T(8,128)(2,1)}, u32[]{:S(2)}, u32[]{:S(2)}) collective-permute-start(bf16[192,768]{1,0:T(8,128)(2,1)S(1)} %copy.24), channel_id=1, source_target_pairs={{240,0},{244,4},{248,8},{252,12},{0,16},{4,20},{8,24},{12,28},{16,... | collective-permute-start | bytes 884744 | tf_op jit(solution)/shard_map/while/body/eval_jaxpr/ppermute | solution.py:12
  145.9 21.1 %copy-start.11 = (f32[64]{0:T(128)S(1)}, f32[64]{0:T(128)}, u32[]{:S(2)}) copy-start(f32[64]{0:T(128)} %param.13) | copy-start | bytes 772
  145.9 21.1 %copy-start.3 = (bf16[768,512]{1,0:T(8,128)(2,1)S(1)}, bf16[768,512]{1,0:T(8,128)(2,1)}, u32[]{:S(2)}) copy-start(bf16[768,512]{1,0:T(8,128)(2,1)} %copy-done.2) | copy-start | bytes 2359300
  146.0 21.1 %copy-start.9 = (bf16[512,64]{0,1:T(8,128)(2,1)S(1)}, bf16[512,64]{0,1:T(8,128)(2,1)}, u32[]{:S(2)}) copy-start(bf16[512,64]{0,1:T(8,128)(2,1)} %param.12) | copy-start | bytes 196612
  148.3 18.7 %all-to-all-start = ((f32[4,64,192]{2,1,0:T(8,128)}), f32[4,64,192]{2,1,0:T(8,128)S(1)}, u32[]{:S(2)}, u32[]{:S(2)}) async-start(f32[4,64,192]{2,1,0:T(8,128)} %bitcast.31), calls=%async_computation | async-start | bytes 524288 | tf_op jit(solution)/shard_map/all_to_all | solution.py:23
  160.3 271.4 %all-reduce.3.cloned.1.call-start = ((), (), s32[]{:S(2)}) async-start(), calls=%async_computation.1 | async-start | bytes 4456448 | tf_op jit(solution)/shard_map/psum | solution.py:119
  (7 other events, 18.9 us)
Sparse Core Ops, SparseCore 0:
  170.1 261.5 all-reduce.2
where the time goes:
time: 445 us; the launch traced here: 442 us
  waiting for transfers between devices  207 us (47%)
  blocking collectives  81.2 us (18%)
  matrix products  68.9 us (15%)
  starting transfers between devices  45.8 us (10%)
  local copies, waits for them, and re-layouts  20.5 us (5%)
  between operations  14.2 us (3%)
    psum x1, waiting for transfers between devices, on_device(): lax.psum((term_w_in, term_b_in, term_w_out), ('blk', 'rep'))  180 us
    psum x1, blocking collectives, on_device(): lax.psum((term_w_in, term_b_in, term_w_out), ('blk', 'rep'))  81.2 us
    ppermute x17, starting transfers between devices, shifted(): return lax.ppermute(block, axis, route)  33.7 us
    dot_general x16, matrix products, couple(): lax.dot_general(own_y, vis_y, (((0,), (0,)), ((), ())), preferred_element...  28.1 us
    dot_general x16, matrix products, couple(): lax.dot_general(vis_y, weight_b, (((1,), (1,)), ((), ())), preferred_elem...  23.8 us
    ppermute x17, waiting for transfers between devices, shifted(): return lax.ppermute(block, axis, route)  20.1 us
    while x14, local copies, waits for them, and re-layouts  13.5 us
    all_to_all x1, starting transfers between devices, sum_at_owner(): lax.all_to_all(cut_along(value, dim, count), axis, 0, 0, tiled=True)  12 us
  transfers between devices with their start and end apart: 19, of which 5 were waited for; matrix products, arithmetic and copies ran while one was open for 14% of the time, Pallas kernels for 0%

commit v1 on v0

--- a/solution.py
+++ b/solution.py
@@ -3,7 +3,165 @@
 import jax
 import jax.numpy as jnp
 from jax import lax
+from jax.experimental import pallas as pl
+from jax.experimental.pallas import tpu as pltpu
 from jax.sharding import PartitionSpec as P
+
+MESH = pl.DeviceIdType.MESH
+F32 = jnp.float32
+BF16 = jnp.bfloat16
+DIN, HID, FEAT, TOK, QUARTER = 1024, 512, 64, 768, 192
+NX, NZ = 4, 8
+ROWS = 144
+NPTS = 49152
+
+
+def dot(a, b, ca, cb):
+    return lax.dot_general(a, b, (((ca,), (cb,)), ((), ())), preferred_element_type=F32)
+
+
+def place():
+    blk = lax.axis_index("blk")
+    rep = lax.axis_index("rep")
+    x = lax.rem(blk, NX)
+    z = lax.rem(lax.div(blk, NX), NZ)
+    y_lo = lax.div(blk, NX * NZ)
+    return x, z, y_lo, lax.div(rep, 2), lax.rem(rep, 2)
+
+
+def device(x, z, y_lo, y_hi, c):
+    return ((y_lo * NZ + z) * NX + x, y_hi * 2 + c)
+
+
+def greet(peers):
+    barrier = pltpu.get_barrier_semaphore()
+    for peer in peers:
+        pl.semaphore_signal(barrier, inc=1, device_id=peer, device_id_type=MESH)
+    pl.semaphore_wait(barrier, len(peers))
+
+
+def grads_kernel(points, hidden, grad, w_out, out, msg, recv_a, stage_b, recv_b, chunk, send_sem, recv_sem):
+    x, z, y_lo, y_hi, c = place()
+    rep = y_hi * 2 + c
+    cell = y_lo * NX + x
+    plane = []
+    column = []
+    for d in range(1, 8):
+        other = lax.rem(cell + d, 8)
+        plane.append((lax.rem(other, NX), lax.div(other, NX)))
+        column.append(lax.rem(z + d, NZ))
+    greet(
+        [device(px, z, py, y_hi, c) for px, py in plane]
+        + [device(x, pz, y_lo, y_hi, c) for pz in column]
+        + [device(x, z, y_lo, 1 - y_hi, c), device(x, z, y_lo, y_hi, 1 - c)]
+    )
+
+    def copy(at, src, dst, peer):
+        return pltpu.make_async_remote_copy(
+            src_ref=src,
+            dst_ref=dst,
+            send_sem=send_sem.at[at],
+            recv_sem=recv_sem.at[at],
+            device_id=peer,
+            device_id_type=MESH,
+        )
+
+    norm = 1.0 / math.sqrt(NPTS)
+    g = grad[...]
+    h32 = hidden[...].astype(F32)
+    pre = dot(g, w_out[...], 0, 1) * (1.0 - h32 * h32)
+    bias = jnp.sum(pre, axis=0, keepdims=True) * norm
+    slab = points[:, pl.ds(pl.multiple_of(rep * 256, 256), 256)]
+    gw = dot(slab, pre.astype(BF16), 0, 0) * norm
+    gwo = dot(grad[pl.ds(pl.multiple_of(rep * 16, 16), 16), :], hidden[...], 1, 0) * norm
+    msg[0, 0:128, :] = gw[0:128].astype(BF16)
+    msg[1, 0:128, :] = gw[128:256].astype(BF16)
+    msg[0, 128:144, :] = gwo.astype(BF16)
+    msg[1, 128:144, :] = jnp.broadcast_to(bias, (16, HID)).astype(BF16)
+
+    def lanes(px):
+        return pl.ds(pl.multiple_of(px * 128, 128), 128)
+
+    copies = []
+    for d in range(1, 8):
+        px, py = plane[d - 1]
+        copies.append(copy(d - 1, msg.at[py, :, lanes(px)], recv_a.at[d - 1], device(px, z, py, y_hi, c)))
+        copies[-1].start()
+    total = msg[y_lo, :, lanes(x)].astype(F32)
+    for d in range(1, 8):
+        copies[d - 1].wait_recv()
+        total = total + recv_a[d - 1].astype(F32)
+    total_b = total.astype(BF16)
+    for b in range(NZ):
+        stage_b[b, 0:16, :] = total_b[b * 16 : b * 16 + 16]
+        stage_b[b, 16:32, :] = total_b[128:144]
+    for d in range(1, 8):
+        pz = column[d - 1]
+        copies.append(copy(6 + d, stage_b.at[pz], recv_b.at[d - 1], device(x, pz, y_lo, y_hi, c)))
+        copies[-1].start()
+    tile = stage_b[z].astype(F32)
+    for d in range(1, 8):
+        copies[6 + d].wait_recv()
+        tile = tile + recv_b[d - 1].astype(F32)
+    tile_b = tile.astype(BF16)
+    mine = pl.ds(pl.multiple_of(z * 16, 16), 16)
+    chunk[mine, :] = tile_b[0:16]
+    chunk[128:144, :] = tile_b[16:32]
+    for d in range(1, 8):
+        pz = column[d - 1]
+        copies.append(copy(13 + d, chunk.at[mine], chunk.at[mine], device(x, pz, y_lo, y_hi, c)))
+        copies[-1].start()
+    for d in range(1, 8):
+        copies[13 + d].wait_recv()
+    out[y_hi, c, y_lo, :, lanes(x)] = chunk[...]
+    place_mine = out.at[y_hi, c, y_lo, :, lanes(x)]
+    copies.append(copy(21, chunk, place_mine, device(x, z, y_lo, 1 - y_hi, c)))
+    copies[21].start()
+    copies[21].wait_recv()
+    pair = out.at[:, c, y_lo, :, lanes(x)]
+    for d in range(1, 8):
+        px, py = plane[d - 1]
+        copies.append(copy(21 + d, pair, pair, device(px, z, py, y_hi, c)))
+        copies[-1].start()
+    for d in range(1, 8):
+        copies[21 + d].wait_recv()
+    half = out.at[:, c]
+    copies.append(copy(29, half, half, device(x, z, y_lo, y_hi, 1 - c)))
+    copies[29].start()
+    copies[29].wait_recv()
+    for one in copies:
+        one.wait_send()
+
+
+def grads(points, hidden, grad, w_out):
+    vmem = pl.BlockSpec(memory_space=pltpu.VMEM)
+    return pl.pallas_call(
+        grads_kernel,
+        out_shape=jax.ShapeDtypeStruct((2, 2, 2, ROWS, HID), BF16),
+        in_specs=[vmem] * 4,
+        out_specs=vmem,
+        scratch_shapes=[
+            pltpu.VMEM((2, ROWS, HID), BF16),
+            pltpu.VMEM((7, ROWS, 128), BF16),
+            pltpu.VMEM((NZ, 32, 128), BF16),
+            pltpu.VMEM((7, 32, 128), BF16),
+            pltpu.VMEM((ROWS, 128), BF16),
+            pltpu.SemaphoreType.DMA((30,)),
+            pltpu.SemaphoreType.DMA((30,)),
+        ],
+        compiler_params=pltpu.CompilerParams(
+            collective_id=1, has_side_effects=True, vmem_limit_bytes=40 << 20
+        ),
+        name="grads",
+    )(points, hidden, grad, w_out)
+
+
+def unpack(table):
+    parts = table.reshape(4, 2, ROWS, HID)
+    grad_w_in = parts[:, :, :128, :].reshape(DIN, HID).astype(F32)
+    grad_b_in = parts[0, 1, 128, :].astype(F32)
+    grad_w_out = parts[:, 0, 128:, :].reshape(FEAT, HID).T.astype(F32)
+    return grad_w_in, grad_b_in, grad_w_out
 
 
 def shifted(block, axis, distance):
@@ -49,11 +207,7 @@
     blocks = lax.axis_size("blk")
     rep_index = lax.axis_index("rep")
     rows = points.shape[0]
-    quarter = rows // reps
-    first = rep_index * quarter
-    npts = rows * blocks
     levels = reps.bit_length() - 1
-    own_points = lax.dynamic_slice_in_dim(points, first, quarter, 0)
     hidden = jnp.tanh(jnp.dot(points, w_in, preferred_element_type=jnp.float32) + b_in).astype(
         jnp.bfloat16
     )
@@ -61,7 +215,6 @@
         w_out, hidden, (((0,), (1,)), ((), ())), preferred_element_type=jnp.float32
     )
     hidden, scaled = (hidden, (pre * inv_scale[:, None]).astype(jnp.bfloat16))
-    own_hidden = lax.dynamic_slice_in_dim(hidden, first, quarter, 0)
     own_pair = jnp.concatenate([solves, probes], axis=0)
     own_sq = jnp.sum(jnp.square(scaled.astype(jnp.float32)), axis=0)
     scaled32 = scaled.astype(jnp.float32)
@@ -94,30 +247,8 @@
     summed = sum_at_owner(drift, "rep", 1)
     feat_grad = summed * inv_scale[:, None]
     grad_b16 = feat_grad.astype(jnp.bfloat16)
-    back = lax.dot_general(
-        grad_b16, w_out, (((0,), (1,)), ((), ())), preferred_element_type=jnp.float32
-    )
-    hid32 = own_hidden.astype(jnp.float32)
-    pre_grad = back * (1.0 - hid32 * hid32)
-    norm = 1.0 / math.sqrt(npts)
-    term_w_in = (
-        lax.dot_general(
-            own_points,
-            pre_grad.astype(jnp.bfloat16),
-            (((0,), (0,)), ((), ())),
-            preferred_element_type=jnp.float32,
-        )
-        * norm
-    )
-    term_b_in = jnp.sum(pre_grad, axis=0) * norm
-    term_w_out = (
-        lax.dot_general(
-            own_hidden, grad_b16, (((0,), (1,)), ((), ())), preferred_element_type=jnp.float32
-        )
-        * norm
-    )
-    grad_w_in, grad_b_in, grad_w_out = lax.psum((term_w_in, term_b_in, term_w_out), ("blk", "rep"))
-    return (feat_grad, grad_w_in, grad_b_in, grad_w_out)
+    whole = lax.all_gather(grad_b16, "rep", axis=1, tiled=True)
+    return (feat_grad, *unpack(grads(points, hidden, whole, w_out)))
 
 
 def solution(mesh):

time: 445 us -> 189 us (0.42)
  waiting for transfers between devices: 207 us -> 32.2 us
  blocking collectives: 81.2 us -> 7.62 us
  Pallas kernels: 0 us -> 36.4 us
  matrix products: 68.9 us -> 53.3 us
  between operations: 14.2 us -> 0.88 us
  local copies, waits for them, and re-layouts: 20.5 us -> 9.42 us
  starting transfers between devices: 45.8 us -> 41.3 us
    psum x1 -> x0, waiting for transfers between devices: 180 us -> none  [on_device(): lax.psum((term_w_in, term_b_in, term_w_out), ('blk', 'rep'))]
    psum x1 -> x0, blocking collectives: 81.2 us -> none  [on_device(): lax.psum((term_w_in, term_b_in, term_w_out), ('blk', 'rep'))]
    pallas_call x0 -> x1, Pallas kernels: none -> 36.4 us  [grads(): pl.pallas_call(grads_kernel, out_shape=jax.ShapeDtypeStruct((2, 2, 2, ROW...]
    while x14, local copies, waits for them, and re-layouts: 13.5 us -> 0.28 us
    all_gather x0 -> x1, blocking collectives: none -> 7.62 us  [on_device(): whole = lax.all_gather(grad_b16, 'rep', axis=1, tiled=True)]
    dot_general x16, matrix products: 28.1 us -> 20.9 us  [couple(): lax.dot_general(own_y, vis_y, (((0,), (0,)), ((), ())), preferred_element...]
    ppermute x17, waiting for transfers between devices: 20.1 us -> 26.4 us  [shifted(): return lax.ppermute(block, axis, route)]
  transfers between devices with their start and end apart: 19 -> 18, of which waited for: 5 -> 10; matrix products, arithmetic and copies ran while one was open for 14% -> 25% of each run, Pallas kernels for 0% -> 0%
where the time goes in v1:
time: 189 us; the launch traced here: 188 us
  matrix products  53.3 us (28%)
  starting transfers between devices  41.3 us (22%)
  Pallas kernels  36.4 us (19%)
  waiting for transfers between devices  32.2 us (17%)
  local copies, waits for them, and re-layouts  9.42 us (5%)
  blocking collectives  7.62 us (4%)
  other arithmetic  6.68 us (4%)
    pallas_call x1, Pallas kernels, grads(): pl.pallas_call(grads_kernel, out_shape=jax.ShapeDtypeStruct((2, 2, 2, ROW...  36.4 us
    ppermute x17, starting transfers between devices, shifted(): return lax.ppermute(block, axis, route)  29.3 us
    ppermute x17, waiting for transfers between devices, shifted(): return lax.ppermute(block, axis, route)  26.4 us
    dot_general x16, matrix products, couple(): lax.dot_general(own_y, vis_y, (((0,), (0,)), ((), ())), preferred_element...  20.9 us
    dot_general x16, matrix products, couple(): lax.dot_general(vis_y, weight_b, (((1,), (1,)), ((), ())), preferred_elem...  20.7 us
    all_to_all x1, starting transfers between devices, sum_at_owner(): lax.all_to_all(cut_along(value, dim, count), axis, 0, 0, tiled=True)  11.9 us
    dot_general x16, matrix products, couple(): lax.dot_general(own_pair, vis_pair, (((0,), (0,)), ((), ())), preferred_e...  8.94 us
    all_gather x1, blocking collectives, on_device(): whole = lax.all_gather(grad_b16, 'rep', axis=1, tiled=True)  7.62 us
  transfers between devices with their start and end apart: 18, of which 10 were waited for; matrix products, arithmetic and copies ran while one was open for 25% of the time, Pallas kernels for 0%

profile of v1, /device:TPU:1, one launch (start us, length us, event | category | flops | bytes accessed | tf_op | source)
XLA Modules:
  0.0 188.2 jit_solution(7053696288856074690)
XLA Ops:
  1.9 2.4 %tanh_convert_fusion.hidden = bf16[768,512]{1,0:T(8,128)(2,1)S(1)} fusion(bf16[768,1024]{1,0:T(8,128)(2,1)} %points.1, bf16[1024,512]{1,0:T(8,128)(2,1)S(1)} %copy-done, f32[512]{0:T(512)} %param.11), kind=kOutput, calls=%fused_computation.24 | convolution fusion | flops 806092800 | bytes 3409920 | tf_op jit(solution)/shard_map/dot_general | solution.py:211
  4.7 9.7 %collective-permute-start.2 = (bf16[192,768]{1,0:T(8,128)(2,1)S(1)}, bf16[192,768]{1,0:T(8,128)(2,1)S(1)}, u32[]{:S(2)}, u32[]{:S(2)}) collective-permute-start(bf16[192,768]{1,0:T(8,128)(2,1)S(1)} %pad_maximum_fusion), channel_id=1, source_target_pairs={{4,0},{8,4},{12,8},{16,12},{20,16},{24,20},{28,24},{32,28},{36,32}... | collective-permute-start | bytes 884744 | tf_op jit(solution)/shard_map/ppermute | solution.py:170
  14.4 5.7 %collective-permute-done.2 = bf16[192,768]{1,0:T(8,128)(2,1)S(1)} collective-permute-done((bf16[192,768]{1,0:T(8,128)(2,1)S(1)}, bf16[192,768]{1,0:T(8,128)(2,1)S(1)}, u32[]{:S(2)}, u32[]{:S(2)}) %collective-permute-start.2) | collective-permute-done | bytes 294944 | tf_op jit(solution)/shard_map/ppermute | solution.py:170
  20.2 2.5 %collective-permute-start.3 = (bf16[192,768]{1,0:T(8,128)(2,1)S(1)}, bf16[192,768]{1,0:T(8,128)(2,1)S(1)}, u32[]{:S(2)}, u32[]{:S(2)}) collective-permute-start(bf16[192,768]{1,0:T(8,128)(2,1)S(1)} %broadcast_select_fusion), channel_id=1, source_target_pairs={{8,0},{12,4},{16,8},{20,12},{24,16},{28,20},{32,24},{36,28},{40,32... | collective-permute-start | bytes 884744 | tf_op jit(solution)/shard_map/ppermute | solution.py:170
  22.7 6.0 %collective-permute-done.3 = bf16[192,768]{1,0:T(8,128)(2,1)S(1)} collective-permute-done((bf16[192,768]{1,0:T(8,128)(2,1)S(1)}, bf16[192,768]{1,0:T(8,128)(2,1)S(1)}, u32[]{:S(2)}, u32[]{:S(2)}) %collective-permute-start.3) | collective-permute-done | bytes 294944 | tf_op jit(solution)/shard_map/ppermute | solution.py:170
  28.9 8.1 %collective-permute-done.4 = bf16[192,768]{1,0:T(8,128)(2,1)S(1)} collective-permute-done((bf16[192,768]{1,0:T(8,128)(2,1)S(1)}, bf16[192,768]{1,0:T(8,128)(2,1)S(1)}, u32[]{:S(2)}, u32[]{:S(2)}) %collective-permute-start.4) | collective-permute-done | bytes 294944 | tf_op jit(solution)/shard_map/ppermute | solution.py:170
  37.0 70.0 %while.17 = (s32[]{:T(128)}, f32[768]{0:T(1024)S(1)}, f32[64,768]{1,0:T(8,128)}, bf16[192,768]{1,0:T(8,128)(2,1)S(1)}, bf16[192,768]{1,0:T(8,128)(2,1)S(1)}, /*i...) while((s32[]{:T(128)}, f32[768]{0:T(1024)S(1)}, ...), condition=%wide.region_6.7_spmd.clone, body=%wide.region_1.6_spmd.clone.sunk | while | flops 613858560 | bytes 20095168 | solution.py:241
  42.9 2.3 %fusion.69 = f32[64,768]{1,0:T(8,128)} fusion(f32[64,768]{1,0:T(8,128)S(1)} %convolution_bitcast_fusion.3, bf16[768,768]{0,1:T(8,128)(2,1)} %get-tuple-element.172, f32[64,768]{1,0:T(8,128)} %get-tuple-element.185, pred[]{:T(512)S(6)} %compare.8, bf16[192,768]{1,0:T(8,128)(2,1)S(1)} %copy.27), kind=kOutput, calls=%fused_computation.7.clone.1 | convolution fusion | flops 75644928 | bytes 1867777 | tf_op jit(solution)/shard_map/while/body/eval_jaxpr/dot_general | solution.py:198
  45.3 2.2 %collective-permute-start = (bf16[192,768]{1,0:T(8,128)(2,1)S(1)}, bf16[192,768]{1,0:T(8,128)(2,1)S(1)}, u32[]{:S(2)}, u32[]{:S(2)}) collective-permute-start(bf16[192,768]{1,0:T(8,128)(2,1)S(1)} %copy.27), channel_id=1, source_target_pairs={{16,0},{20,4},{24,8},{28,12},{32,16},{36,20},{40,24},{44,28},{48,3... | collective-permute-start | bytes 884744 | tf_op jit(solution)/shard_map/while/body/eval_jaxpr/ppermute | solution.py:170
  51.9 2.3 %fusion.69 = f32[64,768]{1,0:T(8,128)} fusion(f32[64,768]{1,0:T(8,128)S(1)} %convolution_bitcast_fusion.3, bf16[768,768]{0,1:T(8,128)(2,1)} %get-tuple-element.172, f32[64,768]{1,0:T(8,128)} %get-tuple-element.185, pred[]{:T(512)S(6)} %compare.8, bf16[192,768]{1,0:T(8,128)(2,1)S(1)} %copy.27), kind=kOutput, calls=%fused_computation.7.clone.1 | convolution fusion | flops 75644928 | bytes 1867777 | tf_op jit(solution)/shard_map/while/body/eval_jaxpr/dot_general | solution.py:198
  55.3 2.5 %collective-permute-start = (bf16[192,768]{1,0:T(8,128)(2,1)S(1)}, bf16[192,768]{1,0:T(8,128)(2,1)S(1)}, u32[]{:S(2)}, u32[]{:S(2)}) collective-permute-start(bf16[192,768]{1,0:T(8,128)(2,1)S(1)} %copy.27), channel_id=1, source_target_pairs={{16,0},{20,4},{24,8},{28,12},{32,16},{36,20},{40,24},{44,28},{48,3... | collective-permute-start | bytes 884744 | tf_op jit(solution)/shard_map/while/body/eval_jaxpr/ppermute | solution.py:170
  62.2 2.3 %fusion.69 = f32[64,768]{1,0:T(8,128)} fusion(f32[64,768]{1,0:T(8,128)S(1)} %convolution_bitcast_fusion.3, bf16[768,768]{0,1:T(8,128)(2,1)} %get-tuple-element.172, f32[64,768]{1,0:T(8,128)} %get-tuple-element.185, pred[]{:T(512)S(6)} %compare.8, bf16[192,768]{1,0:T(8,128)(2,1)S(1)} %copy.27), kind=kOutput, calls=%fused_computation.7.clone.1 | convolution fusion | flops 75644928 | bytes 1867777 | tf_op jit(solution)/shard_map/while/body/eval_jaxpr/dot_general | solution.py:198
  65.6 2.5 %collective-permute-start = (bf16[192,768]{1,0:T(8,128)(2,1)S(1)}, bf16[192,768]{1,0:T(8,128)(2,1)S(1)}, u32[]{:S(2)}, u32[]{:S(2)}) collective-permute-start(bf16[192,768]{1,0:T(8,128)(2,1)S(1)} %copy.27), channel_id=1, source_target_pairs={{16,0},{20,4},{24,8},{28,12},{32,16},{36,20},{40,24},{44,28},{48,3... | collective-permute-start | bytes 884744 | tf_op jit(solution)/shard_map/while/body/eval_jaxpr/ppermute | solution.py:170
  72.6 2.3 %fusion.69 = f32[64,768]{1,0:T(8,128)} fusion(f32[64,768]{1,0:T(8,128)S(1)} %convolution_bitcast_fusion.3, bf16[768,768]{0,1:T(8,128)(2,1)} %get-tuple-element.172, f32[64,768]{1,0:T(8,128)} %get-tuple-element.185, pred[]{:T(512)S(6)} %compare.8, bf16[192,768]{1,0:T(8,128)(2,1)S(1)} %copy.27), kind=kOutput, calls=%fused_computation.7.clone.1 | convolution fusion | flops 75644928 | bytes 1867777 | tf_op jit(solution)/shard_map/while/body/eval_jaxpr/dot_general | solution.py:198
  76.0 2.5 %collective-permute-start = (bf16[192,768]{1,0:T(8,128)(2,1)S(1)}, bf16[192,768]{1,0:T(8,128)(2,1)S(1)}, u32[]{:S(2)}, u32[]{:S(2)}) collective-permute-start(bf16[192,768]{1,0:T(8,128)(2,1)S(1)} %copy.27), channel_id=1, source_target_pairs={{16,0},{20,4},{24,8},{28,12},{32,16},{36,20},{40,24},{44,28},{48,3... | collective-permute-start | bytes 884744 | tf_op jit(solution)/shard_map/while/body/eval_jaxpr/ppermute | solution.py:170
  82.9 2.3 %fusion.69 = f32[64,768]{1,0:T(8,128)} fusion(f32[64,768]{1,0:T(8,128)S(1)} %convolution_bitcast_fusion.3, bf16[768,768]{0,1:T(8,128)(2,1)} %get-tuple-element.172, f32[64,768]{1,0:T(8,128)} %get-tuple-element.185, pred[]{:T(512)S(6)} %compare.8, bf16[192,768]{1,0:T(8,128)(2,1)S(1)} %copy.27), kind=kOutput, calls=%fused_computation.7.clone.1 | convolution fusion | flops 75644928 | bytes 1867777 | tf_op jit(solution)/shard_map/while/body/eval_jaxpr/dot_general | solution.py:198
  86.3 2.5 %collective-permute-start = (bf16[192,768]{1,0:T(8,128)(2,1)S(1)}, bf16[192,768]{1,0:T(8,128)(2,1)S(1)}, u32[]{:S(2)}, u32[]{:S(2)}) collective-permute-start(bf16[192,768]{1,0:T(8,128)(2,1)S(1)} %copy.27), channel_id=1, source_target_pairs={{16,0},{20,4},{24,8},{28,12},{32,16},{36,20},{40,24},{44,28},{48,3... | collective-permute-start | bytes 884744 | tf_op jit(solution)/shard_map/while/body/eval_jaxpr/ppermute | solution.py:170
  93.3 2.3 %fusion.69 = f32[64,768]{1,0:T(8,128)} fusion(f32[64,768]{1,0:T(8,128)S(1)} %convolution_bitcast_fusion.3, bf16[768,768]{0,1:T(8,128)(2,1)} %get-tuple-element.172, f32[64,768]{1,0:T(8,128)} %get-tuple-element.185, pred[]{:T(512)S(6)} %compare.8, bf16[192,768]{1,0:T(8,128)(2,1)S(1)} %copy.27), kind=kOutput, calls=%fused_computation.7.clone.1 | convolution fusion | flops 75644928 | bytes 1867777 | tf_op jit(solution)/shard_map/while/body/eval_jaxpr/dot_general | solution.py:198
  96.7 2.5 %collective-permute-start = (bf16[192,768]{1,0:T(8,128)(2,1)S(1)}, bf16[192,768]{1,0:T(8,128)(2,1)S(1)}, u32[]{:S(2)}, u32[]{:S(2)}) collective-permute-start(bf16[192,768]{1,0:T(8,128)(2,1)S(1)} %copy.27), channel_id=1, source_target_pairs={{16,0},{20,4},{24,8},{28,12},{32,16},{36,20},{40,24},{44,28},{48,3... | collective-permute-start | bytes 884744 | tf_op jit(solution)/shard_map/while/body/eval_jaxpr/ppermute | solution.py:170
  103.6 2.3 %fusion.69 = f32[64,768]{1,0:T(8,128)} fusion(f32[64,768]{1,0:T(8,128)S(1)} %convolution_bitcast_fusion.3, bf16[768,768]{0,1:T(8,128)(2,1)} %get-tuple-element.172, f32[64,768]{1,0:T(8,128)} %get-tuple-element.185, pred[]{:T(512)S(6)} %compare.8, bf16[192,768]{1,0:T(8,128)(2,1)S(1)} %copy.27), kind=kOutput, calls=%fused_computation.7.clone.1 | convolution fusion | flops 75644928 | bytes 1867777 | tf_op jit(solution)/shard_map/while/body/eval_jaxpr/dot_general | solution.py:198
  115.9 11.9 %all-to-all-start = ((f32[4,64,192]{2,1,0:T(8,128)}), f32[4,64,192]{2,1,0:T(8,128)}, u32[]{:S(2)}, u32[]{:S(2)}) async-start(f32[4,64,192]{2,1,0:T(8,128)} %bitcast.73), calls=%async_computation | async-start | bytes 524288 | tf_op jit(solution)/shard_map/all_to_all | solution.py:181
  128.8 5.8 %all-to-all-done = f32[4,64,192]{2,1,0:T(8,128)} async-done(((f32[4,64,192]{2,1,0:T(8,128)}), f32[4,64,192]{2,1,0:T(8,128)}, u32[]{:S(2)}, u32[]{:S(2)}) %all-to-all-start) | async-done | bytes 196640 | tf_op jit(solution)/shard_map/all_to_all | solution.py:181
  137.7 7.6 %all-gather = bf16[4,192,64]{1,2,0:T(8,128)(2,1)S(1)} all-gather(bf16[1,192,64]{1,2,0:T(8,128)(2,1)S(1)} %get-tuple-element.96), channel_id=1, replica_groups=mesh['blk'=64,'rep'=4] {'rep'}, dimensions={0}, use_global_device_ids=true | all-gather | bytes 122880 | tf_op jit(solution)/shard_map/all_gather | solution.py:250
  148.7 36.4 %grads.1 = bf16[2,2,2,144,512]{4,3,2,1,0:T(8,128)(2,1)S(1)} custom-call(bf16[768,1024]{1,0:T(8,128)(2,1)S(1)} %copy-done.1, bf16[768,512]{1,0:T(8,128)(2,1)S(1)} %tanh_convert_fusion.hidden, bf16[64,768]{1,0:T(8,128)(2,1)S(1)} %bitcast.66, bf16[512,64]{1,0:T(8,128)(2,1)S(1)} %copy.15.w_out), custom_call_target="tpu_custom_call" | custom-call | tf_op jit(solution)/shard_map/grads/pallas_call | solution.py:138
  (132 shorter events, 59.7 us)
Async XLA Ops:
  0.6 3.6 %copy-start.7 = (bf16[512,64]{0,1:T(8,128)(2,1)S(1)}, bf16[512,64]{0,1:T(8,128)(2,1)}, u32[]{:S(2)}) copy-start(bf16[512,64]{0,1:T(8,128)(2,1)} %param.12) | copy-start | bytes 196612
  0.7 3.6 %copy-start.8 = (f32[64]{0:T(128)S(1)}, f32[64]{0:T(128)}, u32[]{:S(2)}) copy-start(f32[64]{0:T(128)} %param.13) | copy-start | bytes 772
  0.7 4.0 %copy-start.5 = (bf16[64,768]{1,0:T(8,128)(2,1)S(1)}, bf16[64,768]{1,0:T(8,128)(2,1)}, u32[]{:S(2)}) copy-start(bf16[64,768]{1,0:T(8,128)(2,1)} %param.14) | copy-start | bytes 294916
  1.9 2.8 %copy-start.6 = (bf16[64,768]{1,0:T(8,128)(2,1)S(1)}, bf16[64,768]{1,0:T(8,128)(2,1)}, u32[]{:S(2)}) copy-start(bf16[64,768]{1,0:T(8,128)(2,1)} %param.15) | copy-start | bytes 294916
  4.7 15.4 %collective-permute-start.2 = (bf16[192,768]{1,0:T(8,128)(2,1)S(1)}, bf16[192,768]{1,0:T(8,128)(2,1)S(1)}, u32[]{:S(2)}, u32[]{:S(2)}) collective-permute-start(bf16[192,768]{1,0:T(8,128)(2,1)S(1)} %pad_maximum_fusion), channel_id=1, source_target_pairs={{4,0},{8,4},{12,8},{16,12},{20,16},{24,20},{28,24},{32,28},{36,32}... | collective-permute-start | bytes 884744 | tf_op jit(solution)/shard_map/ppermute | solution.py:170
  20.2 8.5 %collective-permute-start.3 = (bf16[192,768]{1,0:T(8,128)(2,1)S(1)}, bf16[192,768]{1,0:T(8,128)(2,1)S(1)}, u32[]{:S(2)}, u32[]{:S(2)}) collective-permute-start(bf16[192,768]{1,0:T(8,128)(2,1)S(1)} %broadcast_select_fusion), channel_id=1, source_target_pairs={{8,0},{12,4},{16,8},{20,12},{24,16},{28,20},{32,24},{36,28},{40,32... | collective-permute-start | bytes 884744 | tf_op jit(solution)/shard_map/ppermute | solution.py:170
  28.8 8.2 %collective-permute-start.4 = (bf16[192,768]{1,0:T(8,128)(2,1)S(1)}, bf16[192,768]{1,0:T(8,128)(2,1)S(1)}, u32[]{:S(2)}, u32[]{:S(2)}) collective-permute-start(bf16[192,768]{1,0:T(8,128)(2,1)S(1)} %broadcast_select_fusion.1), channel_id=1, source_target_pairs={{240,0},{244,4},{248,8},{252,12},{0,16},{4,20},{8,24},{12,28},{16,... | collective-permute-start | bytes 884744 | tf_op jit(solution)/shard_map/ppermute | solution.py:170
  37.0 8.2 %collective-permute-start = (bf16[192,768]{1,0:T(8,128)(2,1)S(1)}, bf16[192,768]{1,0:T(8,128)(2,1)S(1)}, u32[]{:S(2)}, u32[]{:S(2)}) collective-permute-start(bf16[192,768]{1,0:T(8,128)(2,1)S(1)} %copy.27), channel_id=1, source_target_pairs={{16,0},{20,4},{24,8},{28,12},{32,16},{36,20},{40,24},{44,28},{48,3... | collective-permute-start | bytes 884744 | tf_op jit(solution)/shard_map/while/body/eval_jaxpr/ppermute | solution.py:170
  37.2 8.1 %collective-permute-start.1 = (bf16[192,768]{1,0:T(8,128)(2,1)S(1)}, bf16[192,768]{1,0:T(8,128)(2,1)S(1)}, u32[]{:S(2)}, u32[]{:S(2)}) collective-permute-start(bf16[192,768]{1,0:T(8,128)(2,1)S(1)} %copy.28), channel_id=1, source_target_pairs={{240,0},{244,4},{248,8},{252,12},{0,16},{4,20},{8,24},{12,28},{16,... | collective-permute-start | bytes 884744 | tf_op jit(solution)/shard_map/while/body/eval_jaxpr/ppermute | solution.py:170
  45.3 8.9 %collective-permute-start = (bf16[192,768]{1,0:T(8,128)(2,1)S(1)}, bf16[192,768]{1,0:T(8,128)(2,1)S(1)}, u32[]{:S(2)}, u32[]{:S(2)}) collective-permute-start(bf16[192,768]{1,0:T(8,128)(2,1)S(1)} %copy.27), channel_id=1, source_target_pairs={{16,0},{20,4},{24,8},{28,12},{32,16},{36,20},{40,24},{44,28},{48,3... | collective-permute-start | bytes 884744 | tf_op jit(solution)/shard_map/while/body/eval_jaxpr/ppermute | solution.py:170
  47.5 7.8 %collective-permute-start.1 = (bf16[192,768]{1,0:T(8,128)(2,1)S(1)}, bf16[192,768]{1,0:T(8,128)(2,1)S(1)}, u32[]{:S(2)}, u32[]{:S(2)}) collective-permute-start(bf16[192,768]{1,0:T(8,128)(2,1)S(1)} %copy.28), channel_id=1, source_target_pairs={{240,0},{244,4},{248,8},{252,12},{0,16},{4,20},{8,24},{12,28},{16,... | collective-permute-start | bytes 884744 | tf_op jit(solution)/shard_map/while/body/eval_jaxpr/ppermute | solution.py:170
  55.3 9.2 %collective-permute-start = (bf16[192,768]{1,0:T(8,128)(2,1)S(1)}, bf16[192,768]{1,0:T(8,128)(2,1)S(1)}, u32[]{:S(2)}, u32[]{:S(2)}) collective-permute-start(bf16[192,768]{1,0:T(8,128)(2,1)S(1)} %copy.27), channel_id=1, source_target_pairs={{16,0},{20,4},{24,8},{28,12},{32,16},{36,20},{40,24},{44,28},{48,3... | collective-permute-start | bytes 884744 | tf_op jit(solution)/shard_map/while/body/eval_jaxpr/ppermute | solution.py:170
  57.8 7.8 %collective-permute-start.1 = (bf16[192,768]{1,0:T(8,128)(2,1)S(1)}, bf16[192,768]{1,0:T(8,128)(2,1)S(1)}, u32[]{:S(2)}, u32[]{:S(2)}) collective-permute-start(bf16[192,768]{1,0:T(8,128)(2,1)S(1)} %copy.28), channel_id=1, source_target_pairs={{240,0},{244,4},{248,8},{252,12},{0,16},{4,20},{8,24},{12,28},{16,... | collective-permute-start | bytes 884744 | tf_op jit(solution)/shard_map/while/body/eval_jaxpr/ppermute | solution.py:170
  65.6 9.2 %collective-permute-start = (bf16[192,768]{1,0:T(8,128)(2,1)S(1)}, bf16[192,768]{1,0:T(8,128)(2,1)S(1)}, u32[]{:S(2)}, u32[]{:S(2)}) collective-permute-start(bf16[192,768]{1,0:T(8,128)(2,1)S(1)} %copy.27), channel_id=1, source_target_pairs={{16,0},{20,4},{24,8},{28,12},{32,16},{36,20},{40,24},{44,28},{48,3... | collective-permute-start | bytes 884744 | tf_op jit(solution)/shard_map/while/body/eval_jaxpr/ppermute | solution.py:170
  68.2 7.8 %collective-permute-start.1 = (bf16[192,768]{1,0:T(8,128)(2,1)S(1)}, bf16[192,768]{1,0:T(8,128)(2,1)S(1)}, u32[]{:S(2)}, u32[]{:S(2)}) collective-permute-start(bf16[192,768]{1,0:T(8,128)(2,1)S(1)} %copy.28), channel_id=1, source_target_pairs={{240,0},{244,4},{248,8},{252,12},{0,16},{4,20},{8,24},{12,28},{16,... | collective-permute-start | bytes 884744 | tf_op jit(solution)/shard_map/while/body/eval_jaxpr/ppermute | solution.py:170
  76.0 9.2 %collective-permute-start = (bf16[192,768]{1,0:T(8,128)(2,1)S(1)}, bf16[192,768]{1,0:T(8,128)(2,1)S(1)}, u32[]{:S(2)}, u32[]{:S(2)}) collective-permute-start(bf16[192,768]{1,0:T(8,128)(2,1)S(1)} %copy.27), channel_id=1, source_target_pairs={{16,0},{20,4},{24,8},{28,12},{32,16},{36,20},{40,24},{44,28},{48,3... | collective-permute-start | bytes 884744 | tf_op jit(solution)/shard_map/while/body/eval_jaxpr/ppermute | solution.py:170
  78.5 7.8 %collective-permute-start.1 = (bf16[192,768]{1,0:T(8,128)(2,1)S(1)}, bf16[192,768]{1,0:T(8,128)(2,1)S(1)}, u32[]{:S(2)}, u32[]{:S(2)}) collective-permute-start(bf16[192,768]{1,0:T(8,128)(2,1)S(1)} %copy.28), channel_id=1, source_target_pairs={{240,0},{244,4},{248,8},{252,12},{0,16},{4,20},{8,24},{12,28},{16,... | collective-permute-start | bytes 884744 | tf_op jit(solution)/shard_map/while/body/eval_jaxpr/ppermute | solution.py:170
  86.3 9.2 %collective-permute-start = (bf16[192,768]{1,0:T(8,128)(2,1)S(1)}, bf16[192,768]{1,0:T(8,128)(2,1)S(1)}, u32[]{:S(2)}, u32[]{:S(2)}) collective-permute-start(bf16[192,768]{1,0:T(8,128)(2,1)S(1)} %copy.27), channel_id=1, source_target_pairs={{16,0},{20,4},{24,8},{28,12},{32,16},{36,20},{40,24},{44,28},{48,3... | collective-permute-start | bytes 884744 | tf_op jit(solution)/shard_map/while/body/eval_jaxpr/ppermute | solution.py:170
  88.9 7.8 %collective-permute-start.1 = (bf16[192,768]{1,0:T(8,128)(2,1)S(1)}, bf16[192,768]{1,0:T(8,128)(2,1)S(1)}, u32[]{:S(2)}, u32[]{:S(2)}) collective-permute-start(bf16[192,768]{1,0:T(8,128)(2,1)S(1)} %copy.28), channel_id=1, source_target_pairs={{240,0},{244,4},{248,8},{252,12},{0,16},{4,20},{8,24},{12,28},{16,... | collective-permute-start | bytes 884744 | tf_op jit(solution)/shard_map/while/body/eval_jaxpr/ppermute | solution.py:170
  96.7 9.2 %collective-permute-start = (bf16[192,768]{1,0:T(8,128)(2,1)S(1)}, bf16[192,768]{1,0:T(8,128)(2,1)S(1)}, u32[]{:S(2)}, u32[]{:S(2)}) collective-permute-start(bf16[192,768]{1,0:T(8,128)(2,1)S(1)} %copy.27), channel_id=1, source_target_pairs={{16,0},{20,4},{24,8},{28,12},{32,16},{36,20},{40,24},{44,28},{48,3... | collective-permute-start | bytes 884744 | tf_op jit(solution)/shard_map/while/body/eval_jaxpr/ppermute | solution.py:170
  99.3 7.8 %collective-permute-start.1 = (bf16[192,768]{1,0:T(8,128)(2,1)S(1)}, bf16[192,768]{1,0:T(8,128)(2,1)S(1)}, u32[]{:S(2)}, u32[]{:S(2)}) collective-permute-start(bf16[192,768]{1,0:T(8,128)(2,1)S(1)} %copy.28), channel_id=1, source_target_pairs={{240,0},{244,4},{248,8},{252,12},{0,16},{4,20},{8,24},{12,28},{16,... | collective-permute-start | bytes 884744 | tf_op jit(solution)/shard_map/while/body/eval_jaxpr/ppermute | solution.py:170
  107.0 2.3 %copy-start.3 = (bf16[192,768]{1,0:T(8,128)(2,1)}, bf16[192,768]{1,0:T(8,128)(2,1)S(1)}, u32[]{:S(2)}) copy-start(bf16[192,768]{1,0:T(8,128)(2,1)S(1)} %get-tuple-element.51) | copy-start | bytes 884740
  110.3 37.5 %copy-start.1 = (bf16[768,1024]{1,0:T(8,128)(2,1)S(1)}, bf16[768,1024]{1,0:T(8,128)(2,1)}, u32[]{:S(2)}) copy-start(bf16[768,1024]{1,0:T(8,128)(2,1)} %points.1) | copy-start | bytes 4718596
  115.9 18.7 %all-to-all-start = ((f32[4,64,192]{2,1,0:T(8,128)}), f32[4,64,192]{2,1,0:T(8,128)}, u32[]{:S(2)}, u32[]{:S(2)}) async-start(f32[4,64,192]{2,1,0:T(8,128)} %bitcast.73), calls=%async_computation | async-start | bytes 524288 | tf_op jit(solution)/shard_map/all_to_all | solution.py:181
  (3 other events, 3.1 us)

commit v2 on v1

v2 whole, which is shorter than its diff:
```python
import math

import jax
import jax.numpy as jnp
from jax import lax
from jax.experimental import pallas as pl
from jax.experimental.pallas import tpu as pltpu
from jax.sharding import PartitionSpec as P

MESH = pl.DeviceIdType.MESH
F32 = jnp.float32
BF16 = jnp.bfloat16
DIN, HID, FEAT, TOK, QUARTER = 1024, 512, 64, 768, 192
HALF = TOK // 2
NX, NZ = 4, 8
ROWS = 144
MSG = 192
AUG = 80
NPTS = 49152


def dot(a, b, ca, cb):
    return lax.dot_general(a, b, (((ca,), (cb,)), ((), ())), preferred_element_type=F32)


def place():
    blk = lax.axis_index("blk")
    rep = lax.axis_index("rep")
    x = lax.rem(blk, NX)
    z = lax.rem(lax.div(blk, NX), NZ)
    y_lo = lax.div(blk, NX * NZ)
    return x, z, y_lo, lax.div(rep, 2), lax.rem(rep, 2)


def device(x, z, y_lo, y_hi, c):
    return ((y_lo * NZ + z) * NX + x, y_hi * 2 + c)


def aligned(start, size, step):
    return pl.ds(pl.multiple_of(start, step), size)


def norm_rows(y, ones_first):
    y32 = y.astype(F32)
    half_sq = -0.5 * jnp.sum(y32 * y32, axis=0, keepdims=True)
    high = half_sq.astype(BF16).astype(F32)
    mid = (half_sq - high).astype(BF16).astype(F32)
    low = (half_sq - high - mid).astype(BF16).astype(F32)
    row = lax.broadcasted_iota(jnp.int32, (16, y.shape[1]), 0)
    base = 3 if ones_first else 0
    ones = 0 if ones_first else 3
    rows = jnp.where((row >= ones) & (row < ones + 3), 1.0, 0.0)
    rows = jnp.where(row == base, high, rows)
    rows = jnp.where(row == base + 1, mid, rows)
    rows = jnp.where(row == base + 2, low, rows)
    return rows.astype(BF16)


def kernel(
    points_in, w_in, b_in, w_out, scale, solves, probes,
    feat_out, out,
    points, hidden, own, vis, left, vis_b, vis_y, vis_q, acc, drift, drift_in,
    quart, quart_in, grads, grad, msg, recv_a, stage_b, recv_b, chunk,
    load_sem, send_sem, recv_sem,
):
    x, z, y_lo, y_hi, c = place()
    rep = y_hi * 2 + c
    step = 1 - 2 * c
    cell = y_lo * NX + x
    here = (x, z, y_lo, y_hi, c)
    plane = []
    column = []
    reps = []
    for d in range(1, 8):
        other = lax.rem(cell + d, 8)
        plane.append((lax.rem(other, NX), lax.div(other, NX)))
        column.append(lax.rem(z + d, NZ))
    for d in range(1, 4):
        other = lax.rem(rep + d, 4)
        reps.append((other, device(x, z, y_lo, lax.div(other, 2), lax.rem(other, 2))))
    peers = (
        [device(px, z, py, y_hi, c) for px, py in plane]
        + [device(x, pz, y_lo, y_hi, c) for pz in column]
        + [peer for _, peer in reps]
    )
    x_next = lax.rem(x + step + NX, NX)
    x_prev = lax.rem(x - step + NX, NX)
    x_far = lax.rem(x + 2, NX)
    next_x = device(x_next, z, y_lo, y_hi, c)
    next_z = device(x, lax.rem(z + step + NZ, NZ), y_lo, y_hi, c)
    next_y = device(x, z, 1 - y_lo, y_hi, c)
    twin = device(x, z, y_lo, y_hi, 1 - c)

    def lanes(index):
        return aligned(index * TOK, TOK, TOK)

    def copy(at, src, dst, peer):
        return pltpu.make_async_remote_copy(
            src_ref=src,
            dst_ref=dst,
            send_sem=send_sem.at[at],
            recv_sem=recv_sem.at[at],
            device_id=peer,
            device_id_type=MESH,
        )

    def load(at, src, dst):
        return pltpu.make_async_copy(src, dst, load_sem.at[at])

    loads = [
        load(0, solves, own.at[FEAT : 2 * FEAT, lanes(x)]),
        load(1, probes, own.at[2 * FEAT : MSG, lanes(x)]),
    ]
    base_loads = [
        load(6, solves, vis.at[0, FEAT : 2 * FEAT]),
        load(7, probes, vis.at[0, 2 * FEAT : MSG]),
    ]
    for i in range(4):
        part = slice(i * QUARTER, (i + 1) * QUARTER)
        loads.append(load(2 + i, points_in.at[part], points.at[part]))
    for one in loads:
        one.start()

    @pl.when(y_hi == 0)
    def _():
        for one in base_loads:
            one.start()

    barrier = pltpu.get_barrier_semaphore()
    for peer in peers:
        pl.semaphore_signal(barrier, inc=1, device_id=peer, device_id_type=MESH)
    pl.semaphore_wait(barrier, len(peers))

    pairs = slice(FEAT, MSG)
    feats = slice(0, FEAT)
    kinds = ((0, pairs), (1, feats))

    def to_x(kind):
        at, rows = kinds[kind]
        part = own.at[rows, lanes(x)]
        return copy(at, part, part, next_x)

    def to_x_far(kind):
        size = FEAT if kind == 0 else FEAT // 2
        first = FEAT + c * FEAT if kind == 0 else c * (FEAT // 2)
        part = own.at[aligned(first, size, size), lanes(x_prev)]
        return copy(2 + kind, part, part, next_x)

    def to_twin(kind):
        at, rows = kinds[kind]
        part = own.at[rows, lanes(x_prev)]
        return copy(4 + at, part, part, twin)

    def to_twin_far(kind):
        size = FEAT if kind == 0 else FEAT // 2
        first = FEAT + c * FEAT if kind == 0 else c * (FEAT // 2)
        part = own.at[aligned(first, size, size), lanes(x_far)]
        return copy(6 + kind, part, part, twin)

    def to_y(kind):
        at, rows = kinds[kind]
        return copy(8 + at, own.at[rows, lanes(x)], vis.at[0, rows], next_y)

    def to_z(kind, hop):
        rows = kinds[kind][1]
        return copy(10 + 4 * kind + hop, vis.at[hop, rows], vis.at[hop + 1, rows], next_z)

    def to_z_last(kind):
        rows = kinds[kind][1]
        half = aligned(c * HALF, HALF, HALF)
        return copy(13 + 4 * kind, vis.at[3, rows, half], vis.at[4, rows, half], next_z)

    loads[0].wait()
    loads[1].wait()
    to_x(0).start()

    @pl.when(y_hi == 0)
    def _():
        for one in base_loads:
            one.wait()
        to_z(0, 0).start()

    @pl.when(y_hi == 1)
    def _():
        to_y(0).start()

    for i in range(4):
        part = slice(i * QUARTER, (i + 1) * QUARTER)
        loads[2 + i].wait()
        pre = dot(points[part], w_in[...], 1, 0) + b_in[...]
        hidden[part] = jnp.tanh(pre).astype(BF16)
    scaled = (dot(w_out[...], hidden[...], 0, 1) * scale[...]).astype(BF16)
    own[0:FEAT, lanes(x)] = scaled

    to_x(1).start()

    @pl.when(y_hi == 0)
    def _():
        vis[0, 0:FEAT, :] = scaled
        to_z(1, 0).start()

    @pl.when(y_hi == 1)
    def _():
        to_y(1).start()

    to_x(0).wait_recv()
    to_x_far(0).start()
    to_twin(0).start()

    def ready(index):
        y = own[0:FEAT, lanes(index)]
        left[0:FEAT, lanes(index)] = y
        left[FEAT:AUG, lanes(index)] = norm_rows(y, False)
        left[AUG:128, lanes(index)] = jnp.zeros((128 - AUG, TOK), BF16)

    def derive(slot, first, size):
        at = aligned(first, size, HALF)
        y = vis[slot, 0:FEAT, at]
        augmented = jnp.concatenate([y, norm_rows(y, True)], axis=0)
        vis_b[:, 0:size] = augmented
        padded = jnp.concatenate([augmented, jnp.zeros((128 - AUG, size), BF16)], axis=0)
        vis_y[0:size, :] = padded.T
        swapped = jnp.concatenate([vis[slot, 2 * FEAT : MSG, at], vis[slot, FEAT : 2 * FEAT, at]], axis=0)
        vis_q[0:size, :] = swapped.T

    def couple(i, size):
        exponent = dot(vis_y[0:size, :], left[:, i], 1, 0)
        coupling = dot(vis_q[0:size, :], own[FEAT:MSG, i], 1, 0)
        weight = (coupling * jnp.exp(exponent)).astype(BF16)
        return dot(vis_b[:, 0:size], weight, 1, 0)

    ready(x)

    @pl.when(y_hi == 1)
    def _():
        to_y(0).wait_recv()
        to_z(0, 0).start()
        to_y(1).wait_recv()
        to_z(1, 0).start()

    derive(0, c * HALF, HALF)
    acc[:, lanes(x)] = couple(lanes(x), HALF)
    to_x(1).wait_recv()
    to_x_far(1).start()
    to_twin(1).start()
    to_x_far(0).wait_recv()
    to_twin_far(0).start()
    to_x_far(1).wait_recv()
    to_twin_far(1).start()
    ready(x_prev)
    to_twin(0).wait_recv()
    to_twin(1).wait_recv()
    ready(x_next)
    to_twin_far(0).wait_recv()
    to_twin_far(1).wait_recv()
    ready(x_far)

    def first_tiles(k, carry):
        i = lanes(lax.rem(x + k, NX))
        acc[:, i] = couple(i, HALF)
        return carry

    lax.fori_loop(1, NX, first_tiles, 0)

    def visit(hop, carry):
        to_z(0, hop - 1).wait_recv()
        to_z(1, hop - 1).wait_recv()

        @pl.when(hop < 3)
        def _():
            to_z(0, hop).start()
            to_z(1, hop).start()

        @pl.when(hop == 3)
        def _():
            to_z_last(0).start()
            to_z_last(1).start()

        derive(hop, 0, TOK)

        def tiles(k, inner):
            i = aligned(k * 2 * TOK, 2 * TOK, 2 * TOK)
            acc[:, i] += couple(i, TOK)
            return inner

        return lax.fori_loop(0, 2, tiles, carry)

    lax.fori_loop(1, 4, visit, 0)
    to_z_last(0).wait_recv()
    to_z_last(1).wait_recv()
    derive(4, c * HALF, HALF)

    drifts = []

    def finish(index):
        i = lanes(index)
        pull = acc[:, i] + couple(i, HALF)
        return pull[0:FEAT] - own[0:FEAT, i].astype(F32) * pull[FEAT : FEAT + 1]

    for k in (2, 1, 3):
        index = lax.rem(x + k, NX)
        drift[k - 1] = finish(index).astype(BF16)
        drifts.append(copy(17 + k, drift.at[k - 1], drift_in.at[k - 1], device(index, z, y_lo, y_hi, c)))
        drifts[-1].start()
    total = finish(x)
    for one in drifts:
        one.wait_recv()
    for k in range(3):
        total = total + drift_in[k].astype(F32)
    for q in range(4):
        quart[q] = total[:, q * QUARTER : (q + 1) * QUARTER]
    quarters = []
    for d in range(1, 4):
        other, peer = reps[d - 1]
        quarters.append(copy(20 + d, quart.at[other], quart_in.at[d - 1], peer))
        quarters[-1].start()
    mine = quart[rep]
    for d in range(3):
        quarters[d].wait_recv()
        mine = mine + quart_in[d]
    mine = mine * scale[...]
    feat_out[...] = mine
    grads[rep] = mine.astype(BF16)
    gathers = []
    for d in range(1, 4):
        gathers.append(copy(23 + d, grads.at[rep], grads.at[rep], reps[d - 1][1]))
        gathers[-1].start()
    for one in gathers:
        one.wait_recv()
    for q in range(4):
        grad[:, q * QUARTER : (q + 1) * QUARTER] = grads[q]

    norm = 1.0 / math.sqrt(NPTS)
    h32 = hidden[...].astype(F32)
    pre = dot(grad[...], w_out[...], 0, 1) * (1.0 - h32 * h32)
    bias = jnp.sum(pre, axis=0, keepdims=True) * norm
    slab = points[:, aligned(rep * 256, 256, 256)]
    gw = dot(slab, pre.astype(BF16), 0, 0) * norm
    gwo = dot(grad[aligned(rep * 16, 16, 16), :], hidden[...], 1, 0) * norm
    msg[0, 0:128, :] = gw[0:128].astype(BF16)
    msg[1, 0:128, :] = gw[128:256].astype(BF16)
    msg[0, 128:144, :] = gwo.astype(BF16)
    msg[1, 128:144, :] = jnp.broadcast_to(bias, (16, HID)).astype(BF16)

    def strip(px):
        return aligned(px * 128, 128, 128)

    copies = []
    for d in range(1, 8):
        px, py = plane[d - 1]
        copies.append(copy(26 + d, msg.at[py, :, strip(px)], recv_a.at[d - 1], device(px, z, py, y_hi, c)))
        copies[-1].start()
    summed = msg[y_lo, :, strip(x)].astype(F32)
    for d in range(1, 8):
        copies[d - 1].wait_recv()
        summed = summed + recv_a[d - 1].astype(F32)
    summed_b = summed.astype(BF16)
    for b in range(NZ):
        stage_b[b, 0:16, :] = summed_b[b * 16 : b * 16 + 16]
        stage_b[b, 16:32, :] = summed_b[128:144]
    for d in range(1, 8):
        pz = column[d - 1]
        copies.append(copy(33 + d, stage_b.at[pz], recv_b.at[d - 1], device(x, pz, y_lo, y_hi, c)))
        copies[-1].start()
    tile = stage_b[z].astype(F32)
    for d in range(1, 8):
        copies[6 + d].wait_recv()
        tile = tile + recv_b[d - 1].astype(F32)
    tile_b = tile.astype(BF16)
    band = aligned(z * 16, 16, 16)
    chunk[band, :] = tile_b[0:16]
    chunk[128:144, :] = tile_b[16:32]
    for d in range(1, 8):
        pz = column[d - 1]
        copies.append(copy(40 + d, chunk.at[band], chunk.at[band], device(x, pz, y_lo, y_hi, c)))
        copies[-1].start()
    for d in range(1, 8):
        copies[13 + d].wait_recv()
    out[y_hi, c, y_lo, :, strip(x)] = chunk[...]
    mate = copy(48, chunk, out.at[y_hi, c, y_lo, :, strip(x)], device(x, z, y_lo, 1 - y_hi, c))
    mate.start()
    mate.wait_recv()
    copies.append(mate)
    pair = out.at[:, c, y_lo, :, strip(x)]
    spread = []
    for d in range(1, 8):
        px, py = plane[d - 1]
        spread.append(copy(48 + d, pair, pair, device(px, z, py, y_hi, c)))
        spread[-1].start()
    for one in spread:
        one.wait_recv()
    half = out.at[:, c]
    last = copy(56, half, half, twin)
    last.start()
    last.wait_recv()
    for one in drifts + quarters + gathers + copies + spread + [last]:
        one.wait_send()
    for kind in range(2):
        to_x(kind).wait_send()
        to_x_far(kind).wait_send()
        to_twin(kind).wait_send()
        to_twin_far(kind).wait_send()
        for hop in range(3):
            to_z(kind, hop).wait_send()
        to_z_last(kind).wait_send()

        @pl.when(y_hi == 1)
        def _():
            to_y(kind).wait_send()


def on_device(points, w_in, b_in, w_out, inv_scale, solves, probes):
    vmem = pl.BlockSpec(memory_space=pltpu.VMEM)
    hbm = pl.BlockSpec(memory_space=pl.ANY)
    feat_grad, table = pl.pallas_call(
        kernel,
        out_shape=(
            jax.ShapeDtypeStruct((FEAT, QUARTER), F32),
            jax.ShapeDtypeStruct((2, 2, 2, ROWS, HID), BF16),
        ),
        in_specs=[hbm, vmem, vmem, vmem, vmem, hbm, hbm],
        out_specs=(vmem, vmem),
        scratch_shapes=[
            pltpu.VMEM((TOK, DIN), BF16),
            pltpu.VMEM((TOK, HID), BF16),
            pltpu.VMEM((MSG, NX * TOK), BF16),
            pltpu.VMEM((5, MSG, TOK), BF16),
            pltpu.VMEM((128, NX * TOK), BF16),
            pltpu.VMEM((AUG, TOK), BF16),
            pltpu.VMEM((TOK, 128), BF16),
            pltpu.VMEM((TOK, 128), BF16),
            pltpu.VMEM((AUG, NX * TOK), F32),
            pltpu.VMEM((3, FEAT, TOK), BF16),
            pltpu.VMEM((3, FEAT, TOK), BF16),
            pltpu.VMEM((4, FEAT, QUARTER), F32),
            pltpu.VMEM((3, FEAT, QUARTER), F32),
            pltpu.VMEM((4, FEAT, QUARTER), BF16),
            pltpu.VMEM((FEAT, TOK), BF16),
            pltpu.VMEM((2, ROWS, HID), BF16),
            pltpu.VMEM((7, ROWS, 128), BF16),
            pltpu.VMEM((NZ, 32, 128), BF16),
            pltpu.VMEM((7, 32, 128), BF16),
            pltpu.VMEM((ROWS, 128), BF16),
            pltpu.SemaphoreType.DMA((8,)),
            pltpu.SemaphoreType.DMA((57,)),
            pltpu.SemaphoreType.DMA((57,)),
        ],
        compiler_params=pltpu.CompilerParams(
            collective_id=1, has_side_effects=True, vmem_limit_bytes=56 << 20
        ),
        name="trace_term",
    )(points, w_in, b_in[None, :], w_out, inv_scale[:, None], solves, probes)
    parts = table.reshape(4, 2, ROWS, HID)
    grad_w_in = parts[:, :, :128, :].reshape(DIN, HID).astype(F32)
    grad_b_in = parts[0, 1, 128, :].astype(F32)
    grad_w_out = parts[:, 0, 128:, :].reshape(FEAT, HID).T.astype(F32)
    return feat_grad, grad_w_in, grad_b_in, grad_w_out


def solution(mesh):
    in_specs = (P("blk", None), P(), P(), P(), P(), P(None, "blk"), P(None, "blk"))
    out_specs = (P(None, ("blk", "rep")), P(), P(), P())
    return jax.shard_map(
        on_device, mesh=mesh, in_specs=in_specs, out_specs=out_specs, check_vma=False
    )
```

time: 189 us -> 99.5 us (0.53)
  matrix products: 53.3 us -> 0 us
  Pallas kernels: 36.4 us -> 89.2 us
  starting transfers between devices: 41.3 us -> 0 us
  waiting for transfers between devices: 32.2 us -> 0 us
  blocking collectives: 7.62 us -> 0 us
  local copies, waits for them, and re-layouts: 9.42 us -> 5.76 us
  other arithmetic: 6.68 us -> 3.63 us
    dot_general x50 -> x0, matrix products: 53.3 us -> none  [the longest x16 20.9 us: couple(): lax.dot_general(own_y, vis_y, (((0,), (0,)), ((), ())), preferred_element...]
    pallas_call x1, Pallas kernels: 36.4 us -> 89.2 us  [on_device(): pl.pallas_call(kernel, out_shape=(jax.ShapeDtypeStruct((FEAT, QUARTER), F...]
    ppermute x17 -> x0, starting transfers between devices: 29.3 us -> none  [shifted(): return lax.ppermute(block, axis, route)]
    ppermute x17 -> x0, waiting for transfers between devices: 26.4 us -> none  [shifted(): return lax.ppermute(block, axis, route)]
    all_to_all x1 -> x0, starting transfers between devices: 11.9 us -> none  [sum_at_owner(): lax.all_to_all(cut_along(value, dim, count), axis, 0, 0, tiled=True)]
    all_gather x1 -> x0, blocking collectives: 7.62 us -> none  [on_device(): whole = lax.all_gather(grad_b16, 'rep', axis=1, tiled=True)]
    all_to_all x1 -> x0, waiting for transfers between devices: 5.82 us -> none  [sum_at_owner(): lax.all_to_all(cut_along(value, dim, count), axis, 0, 0, tiled=True)]
    reshape x2 -> x0, local copies, waits for them, and re-layouts: 3.52 us -> none  [cut_along(): value.reshape(*lengths[:dim], count, lengths[dim] // count, *lengths[dim...]
  transfers between devices with their start and end apart: 18 -> 0, of which waited for: 10 -> 0; matrix products, arithmetic and copies ran while one was open for 25% -> 0% of each run, Pallas kernels for 0% -> 0%
where the time goes in v2:
time: 99.5 us; the launch traced here: 99.2 us
  Pallas kernels  89.2 us (90%)
  local copies, waits for them, and re-layouts  5.76 us (6%)
  other arithmetic  3.63 us (4%)
    pallas_call x1, Pallas kernels, on_device(): pl.pallas_call(kernel, out_shape=(jax.ShapeDtypeStruct((FEAT, QUARTER), F...  89.2 us
    unnamed x4, local copies, waits for them, and re-layouts  2.23 us

profile of v2, /device:TPU:1, one launch (start us, length us, event | category | flops | bytes accessed | tf_op | source)
XLA Modules:
  0.0 99.2 jit_solution(16399333808692862260)
XLA Ops:
  0.6 1.4 %copy.12.scale = f32[64,1]{1,0:T(8,128)} copy(f32[64,1]{0,1:T(1,128)} %bitcast.17) | data formatting | bytes 512 | tf_op jit(solution)/shard_map/broadcast_in_dim | solution.py:452
  2.0 1.6 %copy.11.w_out = bf16[512,64]{1,0:T(8,128)(2,1)} copy(bf16[512,64]{0,1:T(8,128)(2,1)} %param.10) | data formatting | bytes 131072 | tf_op args[3]
  3.6 89.2 %trace_term.1 = (f32[64,192]{1,0:T(8,128)}, bf16[2,2,2,144,512]{4,3,2,1,0:T(8,128)(2,1)}) custom-call(bf16[768,1024]{1,0:T(8,128)(2,1)} %points_in.1, bf16[1024,512]{1,0:T(8,128)(2,1)} %w_in.1, f32[1,512]{1,0:T(1,128)} %bitcast.15, bf16[512,64]{1,0:T(8,128)(2,1)} %copy.11.w_out, f32[64,1]{1,0:T(8,128)} %copy.12.scale, bf16[64,768]{1,0:T(8,128)(2,1)} %solves.1, ...), custom_call_target="tpu_custom_call" | custom-call | tf_op jit(solution)/shard_map/trace_term/pallas_call | solution.py:415
  92.7 1.3 %slice_convert_fusion = f32[1,1,1,512]{3,2,1,0:T(1,128)} fusion(bf16[4,2,144,512]{3,2,1,0:T(8,128)(2,1)} %bitcast.12), kind=kLoop, calls=%fused_computation.2 | loop fusion | flops 512 | bytes 3072 | tf_op jit(solution)/shard_map/convert_element_type | solution.py:455
  94.0 0.8 slice.14
  94.9 1.3 %slice.12 = bf16[4,2,128,512]{3,2,1,0:T(8,128)(2,1)S(1)} slice(bf16[4,2,144,512]{3,2,1,0:T(8,128)(2,1)} %bitcast.14), slice={[0:4], [0:2], [0:128], [0:512]} | slice | bytes 2097152 | tf_op jit(solution)/shard_map/slice | solution.py:454
  96.2 0.7 convert_bitcast_fusion
  96.9 0.0 copy-start
  96.9 1.7 %bitcast_convert_fusion = f32[1024,512]{1,0:T(8,128)} fusion(bf16[4,2,128,512]{3,2,1,0:T(8,128)(2,1)S(1)} %slice.12), kind=kLoop, calls=%fused_computation | loop fusion | flops 524288 | bytes 3145728 | tf_op jit(solution)/shard_map/convert_element_type | solution.py:454
  98.6 0.0 copy-done
  98.6 0.6 copy.14
Async XLA Ops:
  96.9 1.7 %copy-start = (f32[64,192]{1,0:T(8,128)S(1)}, f32[64,192]{1,0:T(8,128)}, u32[]{:S(2)}) copy-start(f32[64,192]{1,0:T(8,128)} %get-tuple-element.12) | copy-start | bytes 147460

commit v3 on v1

v3 whole, which is shorter than its diff:
```python
import math

import jax
import jax.numpy as jnp
from jax import lax
from jax.experimental import pallas as pl
from jax.experimental.pallas import tpu as pltpu
from jax.sharding import PartitionSpec as P

MESH = pl.DeviceIdType.MESH
F32 = jnp.float32
BF16 = jnp.bfloat16
DIN, HID, FEAT, TOK, QUARTER = 1024, 512, 64, 768, 192
HALF = TOK // 2
NX, NZ = 4, 8
ROWS = 144
MSG = 192
AUG = 80
NPTS = 49152


def dot(a, b, ca, cb):
    return lax.dot_general(a, b, (((ca,), (cb,)), ((), ())), preferred_element_type=F32)


def place():
    blk = lax.axis_index("blk")
    rep = lax.axis_index("rep")
    x = lax.rem(blk, NX)
    z = lax.rem(lax.div(blk, NX), NZ)
    y_lo = lax.div(blk, NX * NZ)
    return x, z, y_lo, lax.div(rep, 2), lax.rem(rep, 2)


def device(x, z, y_lo, y_hi, c):
    return ((y_lo * NZ + z) * NX + x, y_hi * 2 + c)


def aligned(start, size, step):
    return pl.ds(pl.multiple_of(start, step), size)


def norm_rows(y, ones_first):
    y32 = y.astype(F32)
    half_sq = -0.5 * jnp.sum(y32 * y32, axis=0, keepdims=True)
    high = half_sq.astype(BF16).astype(F32)
    mid = (half_sq - high).astype(BF16).astype(F32)
    low = (half_sq - high - mid).astype(BF16).astype(F32)
    row = lax.broadcasted_iota(jnp.int32, (16, y.shape[1]), 0)
    base = 3 if ones_first else 0
    ones = 0 if ones_first else 3
    rows = jnp.where((row >= ones) & (row < ones + 3), 1.0, 0.0)
    rows = jnp.where(row == base, high, rows)
    rows = jnp.where(row == base + 1, mid, rows)
    rows = jnp.where(row == base + 2, low, rows)
    return rows.astype(BF16)


def kernel(
    points_in, w_in, b_in, w_t, scale_row, solves, probes,
    feat_out, w_in_out, b_in_out, w_out_out,
    points, hidden, slope, slab_t, own, vis, left, vis_b, vis_y, vis_q, acc,
    half_mine, half_out, half_in, part_out, part_in, halves, grad, msg, recv_a, stage_b, recv_b, chunk, table,
    load_sem, send_sem, recv_sem,
):
    x, z, y_lo, y_hi, c = place()
    rep = y_hi * 2 + c
    step = 1 - 2 * c
    y_vis = y_lo + y_hi - 2 * y_lo * y_hi
    x_next = lax.rem(x + step + NX, NX)
    x_prev = lax.rem(x - step + NX, NX)
    x_far = lax.rem(x + 2, NX)
    z_next = lax.rem(z + step + NZ, NZ)
    z_prev = lax.rem(z - step + NZ, NZ)
    twin = device(x, z, y_lo, y_hi, 1 - c)
    next_z = device(x, z_next, y_lo, y_hi, c)
    near = [device(one, z, y_lo, y_hi, c) for one in (x_next, x_prev, x_far)]
    near += [device(x, one, y_lo, y_hi, c) for one in (z_next, z_prev)]
    near += [device(x, one, 1 - y_lo, y_hi, c) for one in (z, z_next, z_prev)]
    near += [twin, device(x, z, y_lo, 1 - y_hi, c)]

    def lanes(index):
        return aligned(index * TOK, TOK, TOK)

    started = []

    def copy(at, src, dst, peer):
        return pltpu.make_async_remote_copy(
            src_ref=src,
            dst_ref=dst,
            send_sem=send_sem.at[at],
            recv_sem=recv_sem.at[at],
            device_id=peer,
            device_id_type=MESH,
        )

    def send(at, src, dst, peer):
        one = copy(at, src, dst, peer)
        one.start()
        started.append(one)
        return one

    def load(at, src, dst):
        return pltpu.make_async_copy(src, dst, load_sem.at[at])

    barrier = pltpu.get_barrier_semaphore()
    for peer in near:
        pl.semaphore_signal(barrier, inc=1, device_id=peer, device_id_type=MESH)
    loads = []
    for i in range(4):
        part = slice(i * QUARTER, (i + 1) * QUARTER)
        loads.append(load(i, points_in.at[part], points.at[part]))
    loads.append(load(4, solves, own.at[FEAT : 2 * FEAT, lanes(x)]))
    loads.append(load(5, probes, own.at[2 * FEAT : MSG, lanes(x)]))
    for one in loads:
        one.start()

    def features(i):
        part = slice(i * QUARTER, (i + 1) * QUARTER)
        loads[i].wait()
        pre = dot(points[part], w_in[...], 1, 0) + b_in[...]
        hidden[part] = jnp.tanh(pre).astype(BF16)

    features(0)
    loads[4].wait()
    loads[5].wait()
    pl.semaphore_wait(barrier, len(near))

    pairs = slice(FEAT, MSG)
    feats = slice(0, FEAT)
    first_half = aligned(c * HALF, HALF, HALF)
    one_side = aligned(FEAT + c * FEAT, FEAT, FEAT)
    x_peers = [device(lax.rem(x + k, NX), z, y_lo, y_hi, c) for k in range(1, 4)]
    visited = device(x, z_next, y_vis, y_hi, c)

    def to_vis(kind, rows):
        return copy(8 + kind, own.at[rows, lanes(x)], vis.at[1, rows], visited)

    def to_base(kind, rows):
        at = aligned(x * TOK + c * HALF, HALF, HALF)
        return copy(10 + kind, own.at[rows, at], vis.at[0, rows, first_half], device(x, z, 1 - y_lo, y_hi, c))

    def to_z(kind, rows, hop):
        return copy(12 + 2 * hop + kind, vis.at[hop, rows], vis.at[hop + 1, rows], next_z)

    def to_z_last(kind, rows):
        return copy(18 + kind, vis.at[3, rows, first_half], vis.at[4, rows, first_half], next_z)

    started.append(to_vis(0, pairs))
    started[-1].start()
    pair_x = []
    for k in (1, 3, 2):
        part = own.at[one_side, lanes(x)]
        pair_x.append((k, send(20 + k, part, part, x_peers[k - 1])))

    @pl.when(y_hi == 1)
    def _():
        to_base(0, pairs).start()

    for i in range(1, 4):
        features(i)
    scale_row_v = scale_row[...]
    eye = lax.broadcasted_iota(jnp.int32, (FEAT, FEAT), 0) == lax.broadcasted_iota(jnp.int32, (FEAT, FEAT), 1)
    scale = jnp.sum(jnp.where(eye, scale_row_v, 0.0), axis=1, keepdims=True)
    scaled = (dot(w_t[...], hidden[...], 1, 1) * scale).astype(BF16)
    own[feats, lanes(x)] = scaled
    started.append(to_vis(1, feats))
    started[-1].start()

    @pl.when(y_hi == 1)
    def _():
        to_base(1, feats).start()

    feat_x = []
    for k in (1, 3, 2):
        part = own.at[feats, lanes(x)]
        feat_x.append((k, send(24 + k, part, part, x_peers[k - 1])))

    @pl.when(y_hi == 0)
    def _():
        vis[0, :, first_half] = own[:, aligned(x * TOK + c * HALF, HALF, HALF)]

    def ready(index):
        y = own[feats, lanes(index)]
        left[feats, lanes(index)] = y
        left[FEAT:AUG, lanes(index)] = norm_rows(y, False)
        left[AUG:128, lanes(index)] = jnp.zeros((128 - AUG, TOK), BF16)

    def derive(slot, first, size, at):
        cols = aligned(first, size, HALF)
        y = vis[slot, feats, cols]
        augmented = jnp.concatenate([y, norm_rows(y, True)], axis=0)
        vis_b[:, at : at + size] = augmented
        padded = jnp.concatenate([augmented, jnp.zeros((128 - AUG, size), BF16)], axis=0)
        vis_y[at : at + size, :] = padded.T
        swapped = jnp.concatenate([vis[slot, 2 * FEAT : MSG, cols], vis[slot, FEAT : 2 * FEAT, cols]], axis=0)
        vis_q[at : at + size, :] = swapped.T

    def couple(i, at, size):
        span = slice(at, at + size)
        exponent = dot(vis_y[span, :], left[:, i], 1, 0)
        coupling = dot(vis_q[span, :], own[pairs, i], 1, 0)
        weight = (coupling * jnp.exp(exponent)).astype(BF16)
        return dot(vis_b[:, span], weight, 1, 0)

    ready(x)
    slab_t[...] = points[:, aligned(rep * 256, 256, 256)].T

    @pl.when(y_hi == 1)
    def _():
        to_base(0, pairs).wait_recv()
        to_base(1, feats).wait_recv()

    derive(0, c * HALF, HALF, 0)
    acc[:, lanes(x)] = couple(lanes(x), 0, HALF)
    twins = []
    for k, one in pair_x:
        one.wait_recv()
        part = own.at[one_side, lanes(lax.rem(x + NX - k, NX))]
        twins.append(send(28 + k, part, part, twin))
    h32 = hidden[...].astype(F32)
    slope[...] = 1.0 - h32 * h32
    to_vis(0, pairs).wait_recv()
    to_z(0, pairs, 1).start()
    to_vis(1, feats).wait_recv()
    to_z(1, feats, 1).start()
    derive(1, 0, TOK, HALF)
    acc[:, lanes(x)] += couple(lanes(x), HALF, TOK)
    for (k, one), mate in zip(feat_x, twins):
        one.wait_recv()
        mate.wait_recv()
        index = lax.rem(x + NX - k, NX)
        ready(index)

    def first_tiles(k, carry):
        i = lanes(lax.rem(x + k, NX))
        acc[:, i] = couple(i, 0, HALF + TOK)
        return carry

    lax.fori_loop(1, NX, first_tiles, 0)
    to_z(0, pairs, 1).wait_recv()
    to_z(1, feats, 1).wait_recv()
    to_z(0, pairs, 2).start()
    to_z(1, feats, 2).start()
    derive(2, 0, TOK, 0)

    def second_tiles(k, carry):
        i = aligned(k * 2 * TOK, 2 * TOK, 2 * TOK)
        acc[:, i] += couple(i, 0, TOK)
        return carry

    lax.fori_loop(0, 2, second_tiles, 0)
    to_z(0, pairs, 2).wait_recv()
    to_z(1, feats, 2).wait_recv()
    to_z_last(0, pairs).start()
    to_z_last(1, feats).start()
    derive(3, 0, TOK, 0)
    to_z_last(0, pairs).wait_recv()
    to_z_last(1, feats).wait_recv()
    derive(4, c * HALF, HALF, TOK)

    half_twin = {}
    parts = []

    def finish(k):
        index = lax.rem(x + k, NX)
        i = lanes(index)
        pull = acc[:, i] + couple(i, 0, TOK + HALF)
        drift = pull[feats] - own[feats, i].astype(F32) * pull[FEAT : FEAT + 1]
        quarter = [drift[:, q * QUARTER : (q + 1) * QUARTER] for q in range(4)]
        first = c == 0
        half_mine[k, :, 0:QUARTER] = jnp.where(first, quarter[0], quarter[1])
        half_mine[k, :, QUARTER:HALF] = jnp.where(first, quarter[2], quarter[3])
        half_out[k, :, 0:QUARTER] = jnp.where(first, quarter[1], quarter[0]).astype(BF16)
        half_out[k, :, QUARTER:HALF] = jnp.where(first, quarter[3], quarter[2]).astype(BF16)
        half_twin[k] = send(32 + k, half_out.at[k], half_in.at[k], twin)

    def pass_on(k):
        half_twin[k].wait_recv()
        part = half_mine[k] + half_in[k].astype(F32)
        part_out[k] = part.astype(BF16)
        index = lax.rem(x + k, NX)
        if k:
            parts.append(send(36 + k, part_out.at[k], part_in.at[k], device(index, z, y_lo, y_hi, c)))
        parts.append(send(40 + k, part_out.at[k], part_in.at[4 + k], device(index, z, y_lo, 1 - y_hi, c)))
        return part

    finish(2)
    finish(1)
    pass_on(2)
    finish(3)
    pass_on(1)
    finish(0)
    pass_on(3)
    total = pass_on(0)
    for one in parts:
        one.wait_recv()
    for k in range(1, 8):
        total = total + part_in[k].astype(F32)
    total = total * scale
    feat_out[...] = jnp.where(y_hi == 0, total[:, 0:QUARTER], total[:, QUARTER:HALF])
    halves[c] = total.astype(BF16)
    send(44, halves.at[c], halves.at[c], twin).wait_recv()
    for q in range(4):
        at = (q // 2) * QUARTER
        grad[:, q * QUARTER : (q + 1) * QUARTER] = halves[q % 2, :, at : at + QUARTER]

    norm = 1.0 / math.sqrt(NPTS)
    pre = dot(grad[...], w_t[...], 0, 0) * slope[...]
    gw = dot(slab_t[...], pre.astype(BF16), 1, 0) * norm
    bias = jnp.sum(pre, axis=0, keepdims=True) * norm
    gwo = dot(grad[aligned(rep * 16, 16, 16), :], hidden[...], 1, 0) * norm
    msg[0, 0:128, :] = gw[0:128].astype(BF16)
    msg[1, 0:128, :] = gw[128:256].astype(BF16)
    msg[0, 128:144, :] = gwo.astype(BF16)
    msg[1, 128:144, :] = jnp.broadcast_to(bias, (16, HID)).astype(BF16)

    def strip(px):
        return aligned(px * 128, 128, 128)

    cell = y_lo * NX + x
    plane = []
    column = []
    for d in range(1, 8):
        other = lax.rem(cell + d, 8)
        plane.append((lax.rem(other, NX), lax.div(other, NX)))
        column.append(lax.rem(z + d, NZ))
    arrivals = []
    for d in range(1, 8):
        px, py = plane[d - 1]
        arrivals.append(send(44 + d, msg.at[py, :, strip(px)], recv_a.at[d - 1], device(px, z, py, y_hi, c)))
    summed = msg[y_lo, :, strip(x)].astype(F32)
    for d in range(1, 8):
        arrivals[d - 1].wait_recv()
        summed = summed + recv_a[d - 1].astype(F32)
    summed_b = summed.astype(BF16)
    for b in range(NZ):
        stage_b[b, 0:16, :] = summed_b[b * 16 : b * 16 + 16]
        stage_b[b, 16:32, :] = summed_b[128:144]
    arrivals = []
    for d in (4, 3, 5, 2, 6, 1, 7):
        pz = column[d - 1]
        arrivals.append(send(51 + d, stage_b.at[pz], recv_b.at[d - 1], device(x, pz, y_lo, y_hi, c)))
    for one in arrivals:
        one.wait_recv()
    tile = stage_b[z].astype(F32)
    for d in range(1, 8):
        tile = tile + recv_b[d - 1].astype(F32)
    tile_b = tile.astype(BF16)
    band = aligned(z * 16, 16, 16)
    chunk[band, :] = tile_b[0:16]
    chunk[128:144, :] = tile_b[16:32]
    arrivals = []
    for d in (4, 3, 5, 2, 6, 1, 7):
        pz = column[d - 1]
        arrivals.append(send(58 + d, chunk.at[band], chunk.at[band], device(x, pz, y_lo, y_hi, c)))
    for one in arrivals:
        one.wait_recv()
    place_mine = table.at[y_hi, c, y_lo, :, strip(x)]
    groups = []
    for dh in range(2):
        for dl in range(2):
            hi = y_hi + dh - 2 * y_hi * dh
            lo = y_lo + dl - 2 * y_lo * dl
            groups.append((dh, dl, hi, lo, []))
    for dx in (2, 1, 3, 0):
        for dh, dl, hi, lo, got in groups[::-1]:
            if dh or dl or dx:
                at = 65 + dh * 8 + dl * 4 + dx
                peer = device(lax.rem(x + dx, NX), z, lo, hi, c)
                got.append(send(at, chunk, place_mine, peer))
    table[y_hi, c, y_lo, :, strip(x)] = chunk[...]
    shared = []
    for dh, dl, hi, lo, got in groups:
        for one in got:
            one.wait_recv()
        part = table.at[hi, c, lo]
        shared.append(send(82 + dh * 2 + dl, part, part, twin))
    for h in range(2):
        for half in range(2):
            row = (h * 2 + c) * 256 + half * 128
            w_in_out[aligned(row, 128, 128), :] = table[h, c, half, 0:128, :]
    for one in shared:
        one.wait_recv()
    for h in range(2):
        for half in range(2):
            row = (h * 2 + 1 - c) * 256 + half * 128
            w_in_out[aligned(row, 128, 128), :] = table[h, 1 - c, half, 0:128, :]
    b_in_out[...] = table[0, 0, 1, 128:144, :].astype(F32)[0:1]
    for q in range(4):
        w_out_out[q * 16 : q * 16 + 16, :] = table[q // 2, q % 2, 0, 128:144, :].astype(F32)
    for one in started:
        one.wait_send()
    for hop in (1, 2):
        to_z(0, pairs, hop).wait_send()
        to_z(1, feats, hop).wait_send()
    to_z_last(0, pairs).wait_send()
    to_z_last(1, feats).wait_send()

    @pl.when(y_hi == 1)
    def _():
        to_base(0, pairs).wait_send()
        to_base(1, feats).wait_send()


def on_device(points, w_in, b_in, w_out, inv_scale, solves, probes):
    vmem = pl.BlockSpec(memory_space=pltpu.VMEM)
    hbm = pl.BlockSpec(memory_space=pl.ANY)
    feat_grad, grad_w_in, grad_b_in, grad_w_out = pl.pallas_call(
        kernel,
        out_shape=(
            jax.ShapeDtypeStruct((FEAT, QUARTER), F32),
            jax.ShapeDtypeStruct((DIN, HID), BF16),
            jax.ShapeDtypeStruct((1, HID), F32),
            jax.ShapeDtypeStruct((FEAT, HID), F32),
        ),
        in_specs=[hbm, vmem, vmem, vmem, vmem, hbm, hbm],
        out_specs=(vmem, vmem, vmem, vmem),
        scratch_shapes=[
            pltpu.VMEM((TOK, DIN), BF16),
            pltpu.VMEM((TOK, HID), BF16),
            pltpu.VMEM((TOK, HID), F32),
            pltpu.VMEM((256, TOK), BF16),
            pltpu.VMEM((MSG, NX * TOK), BF16),
            pltpu.VMEM((5, MSG, TOK), BF16),
            pltpu.VMEM((128, NX * TOK), BF16),
            pltpu.VMEM((AUG, TOK + HALF), BF16),
            pltpu.VMEM((TOK + HALF, 128), BF16),
            pltpu.VMEM((TOK + HALF, 128), BF16),
            pltpu.VMEM((AUG, NX * TOK), F32),
            pltpu.VMEM((4, FEAT, HALF), F32),
            pltpu.VMEM((4, FEAT, HALF), BF16),
            pltpu.VMEM((4, FEAT, HALF), BF16),
            pltpu.VMEM((4, FEAT, HALF), BF16),
            pltpu.VMEM((8, FEAT, HALF), BF16),
            pltpu.VMEM((2, FEAT, HALF), BF16),
            pltpu.VMEM((FEAT, TOK), BF16),
            pltpu.VMEM((2, ROWS, HID), BF16),
            pltpu.VMEM((7, ROWS, 128), BF16),
            pltpu.VMEM((NZ, 32, 128), BF16),
            pltpu.VMEM((7, 32, 128), BF16),
            pltpu.VMEM((ROWS, 128), BF16),
            pltpu.VMEM((2, 2, 2, ROWS, HID), BF16),
            pltpu.SemaphoreType.DMA((6,)),
            pltpu.SemaphoreType.DMA((86,)),
            pltpu.SemaphoreType.DMA((86,)),
        ],
        compiler_params=pltpu.CompilerParams(
            collective_id=1, has_side_effects=True, vmem_limit_bytes=56 << 20
        ),
        name="trace_term",
    )(points, w_in, b_in[None, :], w_out.T, inv_scale[None, :], solves, probes)
    return feat_grad, grad_w_in.astype(F32), grad_b_in[0], grad_w_out.T


def solution(mesh):
    in_specs = (P("blk", None), P(), P(), P(), P(), P(None, "blk"), P(None, "blk"))
    out_specs = (P(None, ("blk", "rep")), P(), P(), P())
    return jax.shard_map(
        on_device, mesh=mesh, in_specs=in_specs, out_specs=out_specs, check_vma=False
    )
```

time: 189 us -> 86.2 us (0.46)
  matrix products: 53.3 us -> 0 us
  Pallas kernels: 36.4 us -> 80.6 us
  starting transfers between devices: 41.3 us -> 0 us
  waiting for transfers between devices: 32.2 us -> 0 us
  blocking collectives: 7.62 us -> 0 us
  local copies, waits for them, and re-layouts: 9.42 us -> 1.88 us
  other arithmetic: 6.68 us -> 2.87 us
    dot_general x50 -> x0, matrix products: 53.3 us -> none  [the longest x16 20.9 us: couple(): lax.dot_general(own_y, vis_y, (((0,), (0,)), ((), ())), preferred_element...]
    pallas_call x1, Pallas kernels: 36.4 us -> 80.6 us  [on_device(): pl.pallas_call(kernel, out_shape=(jax.ShapeDtypeStruct((FEAT, QUARTER), F...]
    ppermute x17 -> x0, starting transfers between devices: 29.3 us -> none  [shifted(): return lax.ppermute(block, axis, route)]
    ppermute x17 -> x0, waiting for transfers between devices: 26.4 us -> none  [shifted(): return lax.ppermute(block, axis, route)]
    all_to_all x1 -> x0, starting transfers between devices: 11.9 us -> none  [sum_at_owner(): lax.all_to_all(cut_along(value, dim, count), axis, 0, 0, tiled=True)]
    all_gather x1 -> x0, blocking collectives: 7.62 us -> none  [on_device(): whole = lax.all_gather(grad_b16, 'rep', axis=1, tiled=True)]
    all_to_all x1 -> x0, waiting for transfers between devices: 5.82 us -> none  [sum_at_owner(): lax.all_to_all(cut_along(value, dim, count), axis, 0, 0, tiled=True)]
    reshape x2 -> x0, local copies, waits for them, and re-layouts: 3.52 us -> none  [cut_along(): value.reshape(*lengths[:dim], count, lengths[dim] // count, *lengths[dim...]
  transfers between devices with their start and end apart: 18 -> 0, of which waited for: 10 -> 0; matrix products, arithmetic and copies ran while one was open for 25% -> 0% of each run, Pallas kernels for 0% -> 0%
where the time goes in v3:
time: 86.2 us; the launch traced here: 86 us
  Pallas kernels  80.6 us (94%)
  other arithmetic  2.87 us (3%)
  local copies, waits for them, and re-layouts  1.88 us (2%)
    pallas_call x1, Pallas kernels, on_device(): pl.pallas_call(kernel, out_shape=(jax.ShapeDtypeStruct((FEAT, QUARTER), F...  80.6 us
    convert_element_type x1, other arithmetic, on_device(): return (feat_grad, grad_w_in.astype(F32), grad_b_in[0], grad_w_out.T)  2.87 us
    unnamed x9, local copies, waits for them, and re-layouts  1.88 us

profile of v3, /device:TPU:1, one launch (start us, length us, event | category | flops | bytes accessed | tf_op | source)
XLA Modules:
  0.0 86.0 jit_solution(4296964355856091858)
XLA Ops:
  0.6 80.6 %trace_term.1 = (f32[64,192]{1,0:T(8,128)}, bf16[1024,512]{1,0:T(8,128)(2,1)}, f32[1,512]{1,0:T(1,128)}, f32[64,512]{1,0:T(8,128)}) custom-call(bf16[768,1024]{1,0:T(8,128)(2,1)} %points_in.1, bf16[1024,512]{1,0:T(8,128)(2,1)} %w_in.1, f32[1,512]{1,0:T(1,128)} %bitcast.8, bf16[64,512]{1,0:T(8,128)(2,1)} %bitcast.6, f32[1,64]{1,0:T(1,128)} %bitcast.9, ...), custom_call_target="tpu_custom_call" | custom-call | tf_op jit(solution)/shard_map/trace_term/pallas_call | solution.py:409
  81.3 0.0 copy-start.1
  81.3 0.0 copy-start.2
  81.3 0.0 copy-start
  81.3 2.9 %convert_element_type.3 = f32[1024,512]{1,0:T(8,128)} convert(bf16[1024,512]{1,0:T(8,128)(2,1)} %get-tuple-element.9) | non-fusion elementwise | flops 524288 | bytes 3145728 | tf_op jit(solution)/shard_map/convert_element_type | solution.py:453
  84.2 0.0 copy-done.1
  84.2 0.6 copy.14
  84.8 0.0 copy-done.2
  84.8 0.6 copy.15
  85.4 0.0 copy-done
  85.4 0.7 copy.16
Async XLA Ops:
  81.3 2.9 %copy-start.1 = (f32[64,192]{1,0:T(8,128)S(1)}, f32[64,192]{1,0:T(8,128)}, u32[]{:S(2)}) copy-start(f32[64,192]{1,0:T(8,128)} %get-tuple-element.16) | copy-start | bytes 147460
  81.3 3.5 %copy-start.2 = (f32[1,512]{1,0:T(1,128)S(1)}, f32[1,512]{1,0:T(1,128)}, u32[]{:S(2)}) copy-start(f32[1,512]{1,0:T(1,128)} %get-tuple-element.10) | copy-start | bytes 6148
  81.3 4.1 %copy-start = (f32[64,512]{1,0:T(8,128)S(1)}, f32[64,512]{1,0:T(8,128)}, u32[]{:S(2)}) copy-start(f32[64,512]{1,0:T(8,128)} %get-tuple-element.11) | copy-start | bytes 393220

commit v4 on v3

--- a/solution.py
+++ b/solution.py
@@ -57,11 +57,11 @@
 
 
 def kernel(
-    points_in, w_in, b_in, w_t, scale_row, solves, probes,
+    points_in, w_in_any, b_in, w_t, scale_row, solves, probes,
     feat_out, w_in_out, b_in_out, w_out_out,
-    points, hidden, slope, slab_t, own, vis, left, vis_b, vis_y, vis_q, acc,
+    points, w_in, hidden, slope, slab_t, own, vis, left, vis_b, vis_y, vis_q, acc,
     half_mine, half_out, half_in, part_out, part_in, halves, grad, msg, recv_a, stage_b, recv_b, chunk, table,
-    load_sem, send_sem, recv_sem,
+    load_sem, send_sem, recv_sem, out_sem,
 ):
     x, z, y_lo, y_hi, c = place()
     rep = y_hi * 2 + c
@@ -110,6 +110,7 @@
     for i in range(4):
         part = slice(i * QUARTER, (i + 1) * QUARTER)
         loads.append(load(i, points_in.at[part], points.at[part]))
+    loads.insert(0, load(6, w_in_any, w_in))
     loads.append(load(4, solves, own.at[FEAT : 2 * FEAT, lanes(x)]))
     loads.append(load(5, probes, own.at[2 * FEAT : MSG, lanes(x)]))
     for one in loads:
@@ -117,13 +118,14 @@
 
     def features(i):
         part = slice(i * QUARTER, (i + 1) * QUARTER)
-        loads[i].wait()
+        loads[i + 1].wait()
         pre = dot(points[part], w_in[...], 1, 0) + b_in[...]
         hidden[part] = jnp.tanh(pre).astype(BF16)
 
+    loads[5].wait()
+    loads[6].wait()
+    loads[0].wait()
     features(0)
-    loads[4].wait()
-    loads[5].wait()
     pl.semaphore_wait(barrier, len(near))
 
     pairs = slice(FEAT, MSG)
@@ -133,30 +135,58 @@
     x_peers = [device(lax.rem(x + k, NX), z, y_lo, y_hi, c) for k in range(1, 4)]
     visited = device(x, z_next, y_vis, y_hi, c)
 
-    def to_vis(kind, rows):
-        return copy(8 + kind, own.at[rows, lanes(x)], vis.at[1, rows], visited)
-
-    def to_base(kind, rows):
+    pieces = [slice(FEAT, 2 * FEAT), slice(2 * FEAT, MSG), feats]
+    vectors = (0, 1)
+    everything = (0, 1, 2)
+
+    def to_vis(n):
+        return copy(n, own.at[pieces[n], lanes(x)], vis.at[1, pieces[n]], visited)
+
+    def to_base(n):
         at = aligned(x * TOK + c * HALF, HALF, HALF)
-        return copy(10 + kind, own.at[rows, at], vis.at[0, rows, first_half], device(x, z, 1 - y_lo, y_hi, c))
-
-    def to_z(kind, rows, hop):
-        return copy(12 + 2 * hop + kind, vis.at[hop, rows], vis.at[hop + 1, rows], next_z)
-
-    def to_z_last(kind, rows):
-        return copy(18 + kind, vis.at[3, rows, first_half], vis.at[4, rows, first_half], next_z)
-
-    started.append(to_vis(0, pairs))
-    started[-1].start()
-    pair_x = []
-    for k in (1, 3, 2):
-        part = own.at[one_side, lanes(x)]
-        pair_x.append((k, send(20 + k, part, part, x_peers[k - 1])))
+        return copy(3 + n, own.at[pieces[n], at], vis.at[0, pieces[n], first_half], device(x, z, 1 - y_lo, y_hi, c))
+
+    def to_z(hop, n):
+        at = 6 + 3 * (hop - 1) + n
+        if hop < 3:
+            return copy(at, vis.at[hop, pieces[n]], vis.at[hop + 1, pieces[n]], next_z)
+        part = (pieces[n], first_half)
+        return copy(at, vis.at[3, *part], vis.at[4, *part], next_z)
+
+    def pump(hop, which):
+        for n in which:
+            (to_vis(n) if hop == 1 else to_z(hop - 1, n)).wait_recv()
+            if hop < 4:
+                started.append(to_z(hop, n))
+                started[-1].start()
 
     @pl.when(y_hi == 1)
     def _():
-        to_base(0, pairs).start()
-
+        for n in vectors:
+            to_base(n).start()
+
+    for n in vectors:
+        started.append(to_vis(n))
+        started[-1].start()
+    pair_x = {}
+    feat_x = {}
+    twins = {}
+
+    def send_pair(k):
+        part = own.at[one_side, lanes(x)]
+        pair_x[k] = send(20 + k, part, part, x_peers[k - 1])
+
+    def send_feat(k):
+        part = own.at[feats, lanes(x)]
+        feat_x[k] = send(24 + k, part, part, x_peers[k - 1])
+
+    def share_pair(k):
+        pair_x[k].wait_recv()
+        part = own.at[one_side, lanes(lax.rem(x + NX - k, NX))]
+        twins[k] = send(28 + k, part, part, twin)
+
+    send_pair(1)
+    send_pair(3)
     for i in range(1, 4):
         features(i)
     scale_row_v = scale_row[...]
@@ -164,17 +194,16 @@
     scale = jnp.sum(jnp.where(eye, scale_row_v, 0.0), axis=1, keepdims=True)
     scaled = (dot(w_t[...], hidden[...], 1, 1) * scale).astype(BF16)
     own[feats, lanes(x)] = scaled
-    started.append(to_vis(1, feats))
-    started[-1].start()
-
     @pl.when(y_hi == 1)
     def _():
-        to_base(1, feats).start()
-
-    feat_x = []
-    for k in (1, 3, 2):
-        part = own.at[feats, lanes(x)]
-        feat_x.append((k, send(24 + k, part, part, x_peers[k - 1])))
+        to_base(2).start()
+
+    started.append(to_vis(2))
+    started[-1].start()
+    send_feat(1)
+    send_feat(3)
+    send_pair(2)
+    send_feat(2)
 
     @pl.when(y_hi == 0)
     def _():
@@ -203,60 +232,47 @@
         weight = (coupling * jnp.exp(exponent)).astype(BF16)
         return dot(vis_b[:, span], weight, 1, 0)
 
+    def meet(k):
+        feat_x[k].wait_recv()
+        twins[k].wait_recv()
+        index = lax.rem(x + NX - k, NX)
+        ready(index)
+        acc[:, lanes(index)] = couple(lanes(index), 0, HALF + TOK)
+
     ready(x)
     slab_t[...] = points[:, aligned(rep * 256, 256, 256)].T
+    h32 = hidden[...].astype(F32)
+    slope[...] = 1.0 - h32 * h32
 
     @pl.when(y_hi == 1)
     def _():
-        to_base(0, pairs).wait_recv()
-        to_base(1, feats).wait_recv()
+        for n in everything:
+            to_base(n).wait_recv()
 
     derive(0, c * HALF, HALF, 0)
     acc[:, lanes(x)] = couple(lanes(x), 0, HALF)
-    twins = []
-    for k, one in pair_x:
-        one.wait_recv()
-        part = own.at[one_side, lanes(lax.rem(x + NX - k, NX))]
-        twins.append(send(28 + k, part, part, twin))
-    h32 = hidden[...].astype(F32)
-    slope[...] = 1.0 - h32 * h32
-    to_vis(0, pairs).wait_recv()
-    to_z(0, pairs, 1).start()
-    to_vis(1, feats).wait_recv()
-    to_z(1, feats, 1).start()
+    share_pair(1)
+    share_pair(3)
+    pump(1, everything)
     derive(1, 0, TOK, HALF)
     acc[:, lanes(x)] += couple(lanes(x), HALF, TOK)
-    for (k, one), mate in zip(feat_x, twins):
-        one.wait_recv()
-        mate.wait_recv()
-        index = lax.rem(x + NX - k, NX)
-        ready(index)
-
-    def first_tiles(k, carry):
-        i = lanes(lax.rem(x + k, NX))
-        acc[:, i] = couple(i, 0, HALF + TOK)
-        return carry
-
-    lax.fori_loop(1, NX, first_tiles, 0)
-    to_z(0, pairs, 1).wait_recv()
-    to_z(1, feats, 1).wait_recv()
-    to_z(0, pairs, 2).start()
-    to_z(1, feats, 2).start()
+    share_pair(2)
+    meet(1)
+    pump(2, vectors)
+    meet(3)
+    pump(2, (2,))
+    meet(2)
     derive(2, 0, TOK, 0)
 
-    def second_tiles(k, carry):
+    def second_tiles(k):
         i = aligned(k * 2 * TOK, 2 * TOK, 2 * TOK)
         acc[:, i] += couple(i, 0, TOK)
-        return carry
-
-    lax.fori_loop(0, 2, second_tiles, 0)
-    to_z(0, pairs, 2).wait_recv()
-    to_z(1, feats, 2).wait_recv()
-    to_z_last(0, pairs).start()
-    to_z_last(1, feats).start()
+
+    second_tiles(0)
+    pump(3, everything)
+    second_tiles(1)
     derive(3, 0, TOK, 0)
-    to_z_last(0, pairs).wait_recv()
-    to_z_last(1, feats).wait_recv()
+    pump(4, everything)
     derive(4, c * HALF, HALF, TOK)
 
     half_twin = {}
@@ -371,42 +387,65 @@
                 got.append(send(at, chunk, place_mine, peer))
     table[y_hi, c, y_lo, :, strip(x)] = chunk[...]
     shared = []
-    for dh, dl, hi, lo, got in groups:
+    stores = []
+
+    def store(at, h, core, half):
+        row = (h * 2 + core) * 256 + half * 128
+        one = pltpu.make_async_copy(table.at[h, core, half, 0:128, :], w_in_out.at[aligned(row, 128, 128), :], out_sem.at[at])
+        one.start()
+        stores.append(one)
+
+    for n, (dh, dl, hi, lo, got) in enumerate(groups):
         for one in got:
             one.wait_recv()
         part = table.at[hi, c, lo]
-        shared.append(send(82 + dh * 2 + dl, part, part, twin))
-    for h in range(2):
-        for half in range(2):
-            row = (h * 2 + c) * 256 + half * 128
-            w_in_out[aligned(row, 128, 128), :] = table[h, c, half, 0:128, :]
-    for one in shared:
-        one.wait_recv()
-    for h in range(2):
-        for half in range(2):
-            row = (h * 2 + 1 - c) * 256 + half * 128
-            w_in_out[aligned(row, 128, 128), :] = table[h, 1 - c, half, 0:128, :]
+        shared.append(send(82 + n, part, part, twin))
+        store(n, hi, c, lo)
+    for n, (dh, dl, hi, lo, got) in enumerate(groups):
+        shared[n].wait_recv()
+        store(4 + n, hi, 1 - c, lo)
     b_in_out[...] = table[0, 0, 1, 128:144, :].astype(F32)[0:1]
     for q in range(4):
         w_out_out[q * 16 : q * 16 + 16, :] = table[q // 2, q % 2, 0, 128:144, :].astype(F32)
     for one in started:
         one.wait_send()
-    for hop in (1, 2):
-        to_z(0, pairs, hop).wait_send()
-        to_z(1, feats, hop).wait_send()
-    to_z_last(0, pairs).wait_send()
-    to_z_last(1, feats).wait_send()
+    for one in stores:
+        one.wait()
 
     @pl.when(y_hi == 1)
     def _():
-        to_base(0, pairs).wait_send()
-        to_base(1, feats).wait_send()
+        for n in everything:
+            to_base(n).wait_send()
+
+
+def write_kernel(feat, w_in, b_in, w_out, feat_out, w_in_out, b_in_out, w_out_out):
+    feat_out[...] = feat[...]
+    w_in_out[...] = w_in[...].astype(F32)
+    b_in_out[...] = b_in[...]
+    w_out_out[...] = w_out[...]
+
+
+def write(feat, w_in, b_in, w_out):
+    specs = []
+    for part in (feat, w_in, b_in, w_out):
+        if part is w_in:
+            specs.append(pl.BlockSpec((DIN // 4, HID), lambda i: (i, 0)))
+        else:
+            specs.append(pl.BlockSpec(part.shape, lambda i: (0, 0)))
+    return pl.pallas_call(
+        write_kernel,
+        grid=(4,),
+        out_shape=tuple(jax.ShapeDtypeStruct(part.shape, F32) for part in (feat, w_in, b_in, w_out)),
+        in_specs=specs,
+        out_specs=tuple(specs),
+        name="write",
+    )(feat, w_in, b_in, w_out)
 
 
 def on_device(points, w_in, b_in, w_out, inv_scale, solves, probes):
     vmem = pl.BlockSpec(memory_space=pltpu.VMEM)
     hbm = pl.BlockSpec(memory_space=pl.ANY)
-    feat_grad, grad_w_in, grad_b_in, grad_w_out = pl.pallas_call(
+    parts = pl.pallas_call(
         kernel,
         out_shape=(
             jax.ShapeDtypeStruct((FEAT, QUARTER), F32),
@@ -414,10 +453,11 @@
             jax.ShapeDtypeStruct((1, HID), F32),
             jax.ShapeDtypeStruct((FEAT, HID), F32),
         ),
-        in_specs=[hbm, vmem, vmem, vmem, vmem, hbm, hbm],
-        out_specs=(vmem, vmem, vmem, vmem),
+        in_specs=[hbm, hbm, vmem, vmem, vmem, hbm, hbm],
+        out_specs=(vmem, hbm, vmem, vmem),
         scratch_shapes=[
             pltpu.VMEM((TOK, DIN), BF16),
+            pltpu.VMEM((DIN, HID), BF16),
             pltpu.VMEM((TOK, HID), BF16),
             pltpu.VMEM((TOK, HID), F32),
             pltpu.VMEM((256, TOK), BF16),
@@ -441,16 +481,18 @@
             pltpu.VMEM((7, 32, 128), BF16),
             pltpu.VMEM((ROWS, 128), BF16),
             pltpu.VMEM((2, 2, 2, ROWS, HID), BF16),
-            pltpu.SemaphoreType.DMA((6,)),
+            pltpu.SemaphoreType.DMA((7,)),
             pltpu.SemaphoreType.DMA((86,)),
             pltpu.SemaphoreType.DMA((86,)),
+            pltpu.SemaphoreType.DMA((8,)),
         ],
         compiler_params=pltpu.CompilerParams(
             collective_id=1, has_side_effects=True, vmem_limit_bytes=56 << 20
         ),
         name="trace_term",
     )(points, w_in, b_in[None, :], w_out.T, inv_scale[None, :], solves, probes)
-    return feat_grad, grad_w_in.astype(F32), grad_b_in[0], grad_w_out.T
+    feat_grad, grad_w_in, grad_b_in, grad_w_out = write(*parts)
+    return feat_grad, grad_w_in, grad_b_in[0], grad_w_out.T
 
 
 def solution(mesh):

time: 86.2 us -> 82.8 us (0.961)
  other arithmetic: 2.87 us -> 0 us
  local copies, waits for them, and re-layouts: 1.88 us -> 0 us
  Pallas kernels: 80.6 us -> 81.9 us
    pallas_call x0 -> x1, Pallas kernels: none -> 3.73 us  [write(): pl.pallas_call(write_kernel, grid=(4,), out_shape=tuple((jax.ShapeDtypeSt...]
    convert_element_type x1 -> x0, other arithmetic: 2.87 us -> none  [on_device(): return (feat_grad, grad_w_in.astype(F32), grad_b_in[0], grad_w_out.T)]
    pallas_call x1, Pallas kernels: 80.6 us -> 78.2 us  [on_device(): pl.pallas_call(kernel, out_shape=(jax.ShapeDtypeStruct((FEAT, QUARTER), F...]
    unnamed x9 -> x0, local copies, waits for them, and re-layouts: 1.88 us -> none
where the time goes in v4:
time: 82.8 us; the launch traced here: 82.6 us
  Pallas kernels  81.9 us (99%)
    pallas_call x1, Pallas kernels, on_device(): pl.pallas_call(kernel, out_shape=(jax.ShapeDtypeStruct((FEAT, QUARTER), F...  78.2 us
    pallas_call x1, Pallas kernels, write(): pl.pallas_call(write_kernel, grid=(4,), out_shape=tuple((jax.ShapeDtypeSt...  3.73 us

profile of v4, /device:TPU:1, one launch (start us, length us, event | category | flops | bytes accessed | tf_op | source)
XLA Modules:
  0.0 82.6 jit_solution(503033557005850596)
XLA Ops:
  0.6 78.2 %trace_term.1 = (f32[64,192]{1,0:T(8,128)}, bf16[1024,512]{1,0:T(8,128)(2,1)}, f32[1,512]{1,0:T(1,128)}, f32[64,512]{1,0:T(8,128)}) custom-call(bf16[768,1024]{1,0:T(8,128)(2,1)} %points_in.1, bf16[1024,512]{1,0:T(8,128)(2,1)} %w_in_any.1, f32[1,512]{1,0:T(1,128)} %bitcast.6, bf16[64,512]{1,0:T(8,128)(2,1)} %bitcast.5, f32[1,64]{1,0:T(1,128)} %bitcast.7, ...), custom_call_target="tpu_custom_call" | custom-call | tf_op jit(solution)/shard_map/trace_term/pallas_call | solution.py:448
  78.8 3.7 %write.1 = (f32[64,192]{1,0:T(8,128)}, f32[1024,512]{1,0:T(8,128)}, f32[1,512]{1,0:T(1,128)}, f32[64,512]{1,0:T(8,128)}) custom-call(f32[64,192]{1,0:T(8,128)} %get-tuple-element.12.feat, bf16[1024,512]{1,0:T(8,128)(2,1)} %get-tuple-element.13.w_in, f32[1,512]{1,0:T(1,128)} %get-tuple-element.14.b_in, f32[64,512]{1,0:T(8,128)} %get-tuple-element.15.w_out), custom_call_target="tpu_custom_call" | custom-call | tf_op jit(solution)/shard_map/write/pallas_call | solution.py:435

commit v5 on v4

--- a/solution.py
+++ b/solution.py
@@ -59,8 +59,8 @@
 def kernel(
     points_in, w_in_any, b_in, w_t, scale_row, solves, probes,
     feat_out, w_in_out, b_in_out, w_out_out,
-    points, w_in, hidden, slope, slab_t, own, vis, left, vis_b, vis_y, vis_q, acc,
-    half_mine, half_out, half_in, part_out, part_in, halves, grad, msg, recv_a, stage_b, recv_b, chunk, table,
+    points, w_in, hidden, slope, slab_t, own, held, vis, mate, left, vis_b, vis_y, vis_q, acc,
+    half_own, part_out, part_in, halves, grad, msg, recv_a, stage_b, recv_b, chunk, table,
     load_sem, send_sem, recv_sem, out_sem,
 ):
     x, z, y_lo, y_hi, c = place()
@@ -80,7 +80,7 @@
     near += [twin, device(x, z, y_lo, 1 - y_hi, c)]
 
     def lanes(index):
-        return aligned(index * TOK, TOK, TOK)
+        return aligned(index * HALF, HALF, HALF)
 
     started = []
 
@@ -111,8 +111,8 @@
         part = slice(i * QUARTER, (i + 1) * QUARTER)
         loads.append(load(i, points_in.at[part], points.at[part]))
     loads.insert(0, load(6, w_in_any, w_in))
-    loads.append(load(4, solves, own.at[FEAT : 2 * FEAT, lanes(x)]))
-    loads.append(load(5, probes, own.at[2 * FEAT : MSG, lanes(x)]))
+    loads.append(load(4, solves, own.at[FEAT : 2 * FEAT]))
+    loads.append(load(5, probes, own.at[2 * FEAT : MSG]))
     for one in loads:
         one.start()
 
@@ -130,28 +130,35 @@
 
     pairs = slice(FEAT, MSG)
     feats = slice(0, FEAT)
-    first_half = aligned(c * HALF, HALF, HALF)
-    one_side = aligned(FEAT + c * FEAT, FEAT, FEAT)
-    x_peers = [device(lax.rem(x + k, NX), z, y_lo, y_hi, c) for k in range(1, 4)]
-    visited = device(x, z_next, y_vis, y_hi, c)
-
     pieces = [slice(FEAT, 2 * FEAT), slice(2 * FEAT, MSG), feats]
     vectors = (0, 1)
     everything = (0, 1, 2)
+    side = aligned(c * HALF, HALF, HALF)
+    x_peers = [device(lax.rem(x + k, NX), z, y_lo, y_hi, c) for k in range(1, 4)]
+    visited = device(x, z_next, y_vis, y_hi, c)
 
     def to_vis(n):
-        return copy(n, own.at[pieces[n], lanes(x)], vis.at[1, pieces[n]], visited)
+        return copy(n, own.at[pieces[n]], vis.at[1, pieces[n]], visited)
 
     def to_base(n):
-        at = aligned(x * TOK + c * HALF, HALF, HALF)
-        return copy(3 + n, own.at[pieces[n], at], vis.at[0, pieces[n], first_half], device(x, z, 1 - y_lo, y_hi, c))
+        return copy(3 + n, own.at[pieces[n], side], vis.at[0, pieces[n], side], device(x, z, 1 - y_lo, y_hi, c))
+
+    def share_base(n):
+        part = vis.at[0, pieces[n], side]
+        return copy(35 + n, part, part, twin)
 
     def to_z(hop, n):
         at = 6 + 3 * (hop - 1) + n
         if hop < 3:
             return copy(at, vis.at[hop, pieces[n]], vis.at[hop + 1, pieces[n]], next_z)
-        part = (pieces[n], first_half)
-        return copy(at, vis.at[3, *part], vis.at[4, *part], next_z)
+        return copy(at, vis.at[3, pieces[n], side], vis.at[4, pieces[n], side], next_z)
+
+    def to_mate(hop, n):
+        at = 23 + 3 * (hop - 1) + n
+        if hop < 4:
+            return copy(at, vis.at[hop, pieces[n]], mate.at[hop - 1, pieces[n]], twin)
+        part = vis.at[4, pieces[n], side]
+        return copy(at, part, part, twin)
 
     def pump(hop, which):
         for n in which:
@@ -159,6 +166,15 @@
             if hop < 4:
                 started.append(to_z(hop, n))
                 started[-1].start()
+            started.append(to_mate(hop, n))
+            started[-1].start()
+
+    def keep_half(rows):
+        for q in range(2):
+            parts = [own[rows, p * QUARTER : (p + 1) * QUARTER] for p in (2 * q, 2 * q + 1)]
+            picked = jnp.where(c == 0, parts[0].astype(F32), parts[1].astype(F32)).astype(BF16)
+            half_own[rows, q * QUARTER : (q + 1) * QUARTER] = picked
+        held[rows, lanes(x)] = half_own[rows, :]
 
     @pl.when(y_hi == 1)
     def _():
@@ -168,147 +184,135 @@
     for n in vectors:
         started.append(to_vis(n))
         started[-1].start()
+    keep_half(pairs)
     pair_x = {}
     feat_x = {}
-    twins = {}
 
     def send_pair(k):
-        part = own.at[one_side, lanes(x)]
-        pair_x[k] = send(20 + k, part, part, x_peers[k - 1])
+        part = held.at[pairs, lanes(x)]
+        pair_x[k] = send(15 + k, part, part, x_peers[k - 1])
 
     def send_feat(k):
-        part = own.at[feats, lanes(x)]
-        feat_x[k] = send(24 + k, part, part, x_peers[k - 1])
-
-    def share_pair(k):
-        pair_x[k].wait_recv()
-        part = own.at[one_side, lanes(lax.rem(x + NX - k, NX))]
-        twins[k] = send(28 + k, part, part, twin)
+        part = held.at[feats, lanes(x)]
+        feat_x[k] = send(19 + k, part, part, x_peers[k - 1])
 
     send_pair(1)
     send_pair(3)
+    send_pair(2)
     for i in range(1, 4):
         features(i)
     scale_row_v = scale_row[...]
     eye = lax.broadcasted_iota(jnp.int32, (FEAT, FEAT), 0) == lax.broadcasted_iota(jnp.int32, (FEAT, FEAT), 1)
     scale = jnp.sum(jnp.where(eye, scale_row_v, 0.0), axis=1, keepdims=True)
     scaled = (dot(w_t[...], hidden[...], 1, 1) * scale).astype(BF16)
-    own[feats, lanes(x)] = scaled
+    own[feats, :] = scaled
     @pl.when(y_hi == 1)
     def _():
         to_base(2).start()
 
     started.append(to_vis(2))
     started[-1].start()
+    keep_half(feats)
     send_feat(1)
     send_feat(3)
-    send_pair(2)
     send_feat(2)
 
     @pl.when(y_hi == 0)
     def _():
-        vis[0, :, first_half] = own[:, aligned(x * TOK + c * HALF, HALF, HALF)]
+        vis[0] = own[...]
 
     def ready(index):
-        y = own[feats, lanes(index)]
+        y = held[feats, lanes(index)]
         left[feats, lanes(index)] = y
         left[FEAT:AUG, lanes(index)] = norm_rows(y, False)
-        left[AUG:128, lanes(index)] = jnp.zeros((128 - AUG, TOK), BF16)
-
-    def derive(slot, first, size, at):
-        cols = aligned(first, size, HALF)
-        y = vis[slot, feats, cols]
+        left[AUG:128, lanes(index)] = jnp.zeros((128 - AUG, HALF), BF16)
+
+    def derive(block, at):
+        span = slice(at, at + TOK)
+        y = block[feats, :]
         augmented = jnp.concatenate([y, norm_rows(y, True)], axis=0)
-        vis_b[:, at : at + size] = augmented
-        padded = jnp.concatenate([augmented, jnp.zeros((128 - AUG, size), BF16)], axis=0)
-        vis_y[at : at + size, :] = padded.T
-        swapped = jnp.concatenate([vis[slot, 2 * FEAT : MSG, cols], vis[slot, FEAT : 2 * FEAT, cols]], axis=0)
-        vis_q[at : at + size, :] = swapped.T
+        vis_b[:, span] = augmented
+        padded = jnp.concatenate([augmented, jnp.zeros((128 - AUG, TOK), BF16)], axis=0)
+        vis_y[span, :] = padded.T
+        swapped = jnp.concatenate([block[2 * FEAT : MSG, :], block[FEAT : 2 * FEAT, :]], axis=0)
+        vis_q[span, :] = swapped.T
 
     def couple(i, at, size):
         span = slice(at, at + size)
         exponent = dot(vis_y[span, :], left[:, i], 1, 0)
-        coupling = dot(vis_q[span, :], own[pairs, i], 1, 0)
+        coupling = dot(vis_q[span, :], held[pairs, i], 1, 0)
         weight = (coupling * jnp.exp(exponent)).astype(BF16)
         return dot(vis_b[:, span], weight, 1, 0)
 
     def meet(k):
         feat_x[k].wait_recv()
-        twins[k].wait_recv()
+        pair_x[k].wait_recv()
         index = lax.rem(x + NX - k, NX)
         ready(index)
-        acc[:, lanes(index)] = couple(lanes(index), 0, HALF + TOK)
+        acc[:, lanes(index)] = couple(lanes(index), 0, TOK)
+
+    def visit(block):
+        derive(block, 0)
+        acc[...] += couple(slice(None), 0, TOK)
+
+    def arrived(hop):
+        for n in everything:
+            to_mate(hop, n).wait_recv()
 
     ready(x)
-    slab_t[...] = points[:, aligned(rep * 256, 256, 256)].T
-    h32 = hidden[...].astype(F32)
-    slope[...] = 1.0 - h32 * h32
 
     @pl.when(y_hi == 1)
     def _():
         for n in everything:
             to_base(n).wait_recv()
-
-    derive(0, c * HALF, HALF, 0)
-    acc[:, lanes(x)] = couple(lanes(x), 0, HALF)
-    share_pair(1)
-    share_pair(3)
-    pump(1, everything)
-    derive(1, 0, TOK, HALF)
-    acc[:, lanes(x)] += couple(lanes(x), HALF, TOK)
-    share_pair(2)
+            share_base(n).start()
+        for n in everything:
+            share_base(n).wait_recv()
+
+    derive(vis.at[0], 0)
+    acc[:, lanes(x)] = couple(lanes(x), 0, TOK)
+    slab_t[...] = points[:, aligned(rep * 256, 256, 256)].T
+    h32 = hidden[...].astype(F32)
+    slope[...] = 1.0 - h32 * h32
+    pump(1, vectors)
     meet(1)
+    pump(1, (2,))
+    meet(3)
+    meet(2)
+    visit(vis.at[1])
     pump(2, vectors)
-    meet(3)
+    arrived(1)
+    visit(mate.at[0])
     pump(2, (2,))
-    meet(2)
-    derive(2, 0, TOK, 0)
-
-    def second_tiles(k):
-        i = aligned(k * 2 * TOK, 2 * TOK, 2 * TOK)
-        acc[:, i] += couple(i, 0, TOK)
-
-    second_tiles(0)
-    pump(3, everything)
-    second_tiles(1)
-    derive(3, 0, TOK, 0)
+    visit(vis.at[2])
+    pump(3, vectors)
+    arrived(2)
+    visit(mate.at[1])
+    pump(3, (2,))
+    visit(vis.at[3])
     pump(4, everything)
-    derive(4, c * HALF, HALF, TOK)
-
-    half_twin = {}
+    arrived(3)
+    derive(mate.at[2], 0)
+    arrived(4)
+    derive(vis.at[4], TOK)
+
     parts = []
 
     def finish(k):
         index = lax.rem(x + k, NX)
         i = lanes(index)
-        pull = acc[:, i] + couple(i, 0, TOK + HALF)
-        drift = pull[feats] - own[feats, i].astype(F32) * pull[FEAT : FEAT + 1]
-        quarter = [drift[:, q * QUARTER : (q + 1) * QUARTER] for q in range(4)]
-        first = c == 0
-        half_mine[k, :, 0:QUARTER] = jnp.where(first, quarter[0], quarter[1])
-        half_mine[k, :, QUARTER:HALF] = jnp.where(first, quarter[2], quarter[3])
-        half_out[k, :, 0:QUARTER] = jnp.where(first, quarter[1], quarter[0]).astype(BF16)
-        half_out[k, :, QUARTER:HALF] = jnp.where(first, quarter[3], quarter[2]).astype(BF16)
-        half_twin[k] = send(32 + k, half_out.at[k], half_in.at[k], twin)
-
-    def pass_on(k):
-        half_twin[k].wait_recv()
-        part = half_mine[k] + half_in[k].astype(F32)
-        part_out[k] = part.astype(BF16)
-        index = lax.rem(x + k, NX)
+        pull = acc[:, i] + couple(i, 0, 2 * TOK)
+        drift = pull[feats] - held[feats, i].astype(F32) * pull[FEAT : FEAT + 1]
+        part_out[k] = drift.astype(BF16)
+        parts.append(send(41 + k, part_out.at[k], part_in.at[4 + k], device(index, z, y_lo, 1 - y_hi, c)))
         if k:
-            parts.append(send(36 + k, part_out.at[k], part_in.at[k], device(index, z, y_lo, y_hi, c)))
-        parts.append(send(40 + k, part_out.at[k], part_in.at[4 + k], device(index, z, y_lo, 1 - y_hi, c)))
-        return part
+            parts.append(send(37 + k, part_out.at[k], part_in.at[k], device(index, z, y_lo, y_hi, c)))
+        return drift
 
     finish(2)
     finish(1)
-    pass_on(2)
     finish(3)
-    pass_on(1)
-    finish(0)
-    pass_on(3)
-    total = pass_on(0)
+    total = finish(0)
     for one in parts:
         one.wait_recv()
     for k in range(1, 8):
@@ -316,7 +320,7 @@
     total = total * scale
     feat_out[...] = jnp.where(y_hi == 0, total[:, 0:QUARTER], total[:, QUARTER:HALF])
     halves[c] = total.astype(BF16)
-    send(44, halves.at[c], halves.at[c], twin).wait_recv()
+    send(86, halves.at[c], halves.at[c], twin).wait_recv()
     for q in range(4):
         at = (q // 2) * QUARTER
         grad[:, q * QUARTER : (q + 1) * QUARTER] = halves[q % 2, :, at : at + QUARTER]
@@ -416,6 +420,7 @@
     def _():
         for n in everything:
             to_base(n).wait_send()
+            share_base(n).wait_send()
 
 
 def write_kernel(feat, w_in, b_in, w_out, feat_out, w_in_out, b_in_out, w_out_out):
@@ -461,16 +466,16 @@
             pltpu.VMEM((TOK, HID), BF16),
             pltpu.VMEM((TOK, HID), F32),
             pltpu.VMEM((256, TOK), BF16),
-            pltpu.VMEM((MSG, NX * TOK), BF16),
+            pltpu.VMEM((MSG, TOK), BF16),
+            pltpu.VMEM((MSG, NX * HALF), BF16),
             pltpu.VMEM((5, MSG, TOK), BF16),
-            pltpu.VMEM((128, NX * TOK), BF16),
-            pltpu.VMEM((AUG, TOK + HALF), BF16),
-            pltpu.VMEM((TOK + HALF, 128), BF16),
-            pltpu.VMEM((TOK + HALF, 128), BF16),
-            pltpu.VMEM((AUG, NX * TOK), F32),
-            pltpu.VMEM((4, FEAT, HALF), F32),
-            pltpu.VMEM((4, FEAT, HALF), BF16),
-            pltpu.VMEM((4, FEAT, HALF), BF16),
+            pltpu.VMEM((3, MSG, TOK), BF16),
+            pltpu.VMEM((128, NX * HALF), BF16),
+            pltpu.VMEM((AUG, 2 * TOK), BF16),
+            pltpu.VMEM((2 * TOK, 128), BF16),
+            pltpu.VMEM((2 * TOK, 128), BF16),
+            pltpu.VMEM((AUG, NX * HALF), F32),
+            pltpu.VMEM((MSG, HALF), BF16),
             pltpu.VMEM((4, FEAT, HALF), BF16),
             pltpu.VMEM((8, FEAT, HALF), BF16),
             pltpu.VMEM((2, FEAT, HALF), BF16),
@@ -482,8 +487,8 @@
             pltpu.VMEM((ROWS, 128), BF16),
             pltpu.VMEM((2, 2, 2, ROWS, HID), BF16),
             pltpu.SemaphoreType.DMA((7,)),
-            pltpu.SemaphoreType.DMA((86,)),
-            pltpu.SemaphoreType.DMA((86,)),
+            pltpu.SemaphoreType.DMA((87,)),
+            pltpu.SemaphoreType.DMA((87,)),
             pltpu.SemaphoreType.DMA((8,)),
         ],
         compiler_params=pltpu.CompilerParams(

time: 82.8 us -> 81 us (0.978)
  Pallas kernels: 81.9 us -> 80.1 us
    pallas_call x1, Pallas kernels: 78.2 us -> 76.4 us  [on_device(): pl.pallas_call(kernel, out_shape=(jax.ShapeDtypeStruct((FEAT, QUARTER), F...]
where the time goes in v5:
time: 81 us; the launch traced here: 80.8 us
  Pallas kernels  80.1 us (99%)
    pallas_call x1, Pallas kernels, on_device(): pl.pallas_call(kernel, out_shape=(jax.ShapeDtypeStruct((FEAT, QUARTER), F...  76.4 us
    pallas_call x1, Pallas kernels, write(): pl.pallas_call(write_kernel, grid=(4,), out_shape=tuple((jax.ShapeDtypeSt...  3.73 us

profile of v5, /device:TPU:1, one launch (start us, length us, event | category | flops | bytes accessed | tf_op | source)
XLA Modules:
  0.0 80.8 jit_solution(12063893750733809072)
XLA Ops:
  0.6 76.4 %trace_term.1 = (f32[64,192]{1,0:T(8,128)}, bf16[1024,512]{1,0:T(8,128)(2,1)}, f32[1,512]{1,0:T(1,128)}, f32[64,512]{1,0:T(8,128)}) custom-call(bf16[768,1024]{1,0:T(8,128)(2,1)} %points_in.1, bf16[1024,512]{1,0:T(8,128)(2,1)} %w_in_any.1, f32[1,512]{1,0:T(1,128)} %bitcast.6, bf16[64,512]{1,0:T(8,128)(2,1)} %bitcast.5, f32[1,64]{1,0:T(1,128)} %bitcast.7, ...), custom_call_target="tpu_custom_call" | custom-call | tf_op jit(solution)/shard_map/trace_term/pallas_call | solution.py:453
  77.0 3.7 %write.1 = (f32[64,192]{1,0:T(8,128)}, f32[1024,512]{1,0:T(8,128)}, f32[1,512]{1,0:T(1,128)}, f32[64,512]{1,0:T(8,128)}) custom-call(f32[64,192]{1,0:T(8,128)} %get-tuple-element.12.feat, bf16[1024,512]{1,0:T(8,128)(2,1)} %get-tuple-element.13.w_in, f32[1,512]{1,0:T(1,128)} %get-tuple-element.14.b_in, f32[64,512]{1,0:T(8,128)} %get-tuple-element.15.w_out), custom_call_target="tpu_custom_call" | custom-call | tf_op jit(solution)/shard_map/write/pallas_call | solution.py:440

commit v6 on v5

--- a/solution.py
+++ b/solution.py
@@ -106,25 +106,25 @@
     barrier = pltpu.get_barrier_semaphore()
     for peer in near:
         pl.semaphore_signal(barrier, inc=1, device_id=peer, device_id_type=MESH)
-    loads = []
-    for i in range(4):
-        part = slice(i * QUARTER, (i + 1) * QUARTER)
-        loads.append(load(i, points_in.at[part], points.at[part]))
-    loads.insert(0, load(6, w_in_any, w_in))
-    loads.append(load(4, solves, own.at[FEAT : 2 * FEAT]))
-    loads.append(load(5, probes, own.at[2 * FEAT : MSG]))
+    loads = [
+        load(0, solves, own.at[FEAT : 2 * FEAT]),
+        load(1, probes, own.at[2 * FEAT : MSG]),
+        load(2, w_in_any, w_in),
+    ]
+    for i in range(2):
+        part = slice(i * HALF, (i + 1) * HALF)
+        loads.append(load(3 + i, points_in.at[part], points.at[part]))
     for one in loads:
         one.start()
 
     def features(i):
-        part = slice(i * QUARTER, (i + 1) * QUARTER)
-        loads[i + 1].wait()
+        part = slice(i * HALF, (i + 1) * HALF)
+        loads[3 + i].wait()
         pre = dot(points[part], w_in[...], 1, 0) + b_in[...]
         hidden[part] = jnp.tanh(pre).astype(BF16)
 
-    loads[5].wait()
-    loads[6].wait()
-    loads[0].wait()
+    for one in loads[:3]:
+        one.wait()
     features(0)
     pl.semaphore_wait(barrier, len(near))
 
@@ -199,8 +199,7 @@
     send_pair(1)
     send_pair(3)
     send_pair(2)
-    for i in range(1, 4):
-        features(i)
+    features(1)
     scale_row_v = scale_row[...]
     eye = lax.broadcasted_iota(jnp.int32, (FEAT, FEAT), 0) == lax.broadcasted_iota(jnp.int32, (FEAT, FEAT), 1)
     scale = jnp.sum(jnp.where(eye, scale_row_v, 0.0), axis=1, keepdims=True)
@@ -274,10 +273,10 @@
     slab_t[...] = points[:, aligned(rep * 256, 256, 256)].T
     h32 = hidden[...].astype(F32)
     slope[...] = 1.0 - h32 * h32
+    meet(1)
     pump(1, vectors)
-    meet(1)
+    meet(3)
     pump(1, (2,))
-    meet(3)
     meet(2)
     visit(vis.at[1])
     pump(2, vectors)
@@ -327,32 +326,33 @@
 
     norm = 1.0 / math.sqrt(NPTS)
     pre = dot(grad[...], w_t[...], 0, 0) * slope[...]
-    gw = dot(slab_t[...], pre.astype(BF16), 1, 0) * norm
-    bias = jnp.sum(pre, axis=0, keepdims=True) * norm
-    gwo = dot(grad[aligned(rep * 16, 16, 16), :], hidden[...], 1, 0) * norm
-    msg[0, 0:128, :] = gw[0:128].astype(BF16)
-    msg[1, 0:128, :] = gw[128:256].astype(BF16)
-    msg[0, 128:144, :] = gwo.astype(BF16)
-    msg[1, 128:144, :] = jnp.broadcast_to(bias, (16, HID)).astype(BF16)
-
+    pre_b = pre.astype(BF16)
     def strip(px):
         return aligned(px * 128, 128, 128)
 
-    cell = y_lo * NX + x
-    plane = []
     column = []
     for d in range(1, 8):
-        other = lax.rem(cell + d, 8)
-        plane.append((lax.rem(other, NX), lax.div(other, NX)))
         column.append(lax.rem(z + d, NZ))
     arrivals = []
-    for d in range(1, 8):
-        px, py = plane[d - 1]
-        arrivals.append(send(44 + d, msg.at[py, :, strip(px)], recv_a.at[d - 1], device(px, z, py, y_hi, c)))
+
+    def scatter(row, first):
+        msg[row, 0:128, :] = (dot(slab_t[aligned(row * 128, 128, 128), :], pre_b, 1, 0) * norm).astype(BF16)
+        small = jnp.where(row == 0, gwo, bias)
+        msg[row, 128:144, :] = small.astype(BF16)
+        for dx in (2, 1, 3) if first is None else (2, 1, 3, 0):
+            px = lax.rem(x + dx, NX)
+            at = (first or 0) + dx
+            arrivals.append(send(45 + at, msg.at[row, :, strip(px)], recv_a.at[at], device(px, z, row, y_hi, c)))
+
+    gwo = dot(grad[aligned(rep * 16, 16, 16), :], hidden[...], 1, 0) * norm
+    bias = jnp.broadcast_to(jnp.sum(pre, axis=0, keepdims=True) * norm, (16, HID))
+    scatter(1 - y_lo, 4)
+    scatter(y_lo, None)
     summed = msg[y_lo, :, strip(x)].astype(F32)
-    for d in range(1, 8):
-        arrivals[d - 1].wait_recv()
-        summed = summed + recv_a[d - 1].astype(F32)
+    for one in arrivals:
+        one.wait_recv()
+    for at in range(1, 8):
+        summed = summed + recv_a[at].astype(F32)
     summed_b = summed.astype(BF16)
     for b in range(NZ):
         stage_b[b, 0:16, :] = summed_b[b * 16 : b * 16 + 16]
@@ -360,7 +360,7 @@
     arrivals = []
     for d in (4, 3, 5, 2, 6, 1, 7):
         pz = column[d - 1]
-        arrivals.append(send(51 + d, stage_b.at[pz], recv_b.at[d - 1], device(x, pz, y_lo, y_hi, c)))
+        arrivals.append(send(87 + d, stage_b.at[pz], recv_b.at[d - 1], device(x, pz, y_lo, y_hi, c)))
     for one in arrivals:
         one.wait_recv()
     tile = stage_b[z].astype(F32)
@@ -423,33 +423,47 @@
             share_base(n).wait_send()
 
 
-def write_kernel(feat, w_in, b_in, w_out, feat_out, w_in_out, b_in_out, w_out_out):
-    feat_out[...] = feat[...]
-    w_in_out[...] = w_in[...].astype(F32)
-    b_in_out[...] = b_in[...]
-    w_out_out[...] = w_out[...]
+def write_kernel(feat, w_in, b_in, w_out, feat_out, w_in_out, b_in_out, w_out_out, narrow, wide, load_sem, store_sem):
+    count = 8
+    rows = [slice(i * DIN // count, (i + 1) * DIN // count) for i in range(count)]
+    loads = [pltpu.make_async_copy(w_in.at[r], narrow.at[r], load_sem.at[i]) for i, r in enumerate(rows)]
+    stores = [pltpu.make_async_copy(wide.at[r], w_in_out.at[r], store_sem.at[i]) for i, r in enumerate(rows)]
+    for one in loads:
+        one.start()
+    pairs = ((feat, feat_out), (b_in, b_in_out), (w_out, w_out_out))
+    small = [pltpu.make_async_copy(src, dst, store_sem.at[count + i]) for i, (src, dst) in enumerate(pairs)]
+    for one in small:
+        one.start()
+    for i, r in enumerate(rows):
+        loads[i].wait()
+        wide[r] = narrow[r].astype(F32)
+        stores[i].start()
+    for one in small + stores:
+        one.wait()
 
 
 def write(feat, w_in, b_in, w_out):
-    specs = []
-    for part in (feat, w_in, b_in, w_out):
-        if part is w_in:
-            specs.append(pl.BlockSpec((DIN // 4, HID), lambda i: (i, 0)))
-        else:
-            specs.append(pl.BlockSpec(part.shape, lambda i: (0, 0)))
+    free = pl.BlockSpec(memory_space=pl.ANY)
     return pl.pallas_call(
         write_kernel,
-        grid=(4,),
         out_shape=tuple(jax.ShapeDtypeStruct(part.shape, F32) for part in (feat, w_in, b_in, w_out)),
-        in_specs=specs,
-        out_specs=tuple(specs),
+        in_specs=[free] * 4,
+        out_specs=(free,) * 4,
+        scratch_shapes=[
+            pltpu.VMEM((DIN, HID), BF16),
+            pltpu.VMEM((DIN, HID), F32),
+            pltpu.SemaphoreType.DMA((8,)),
+            pltpu.SemaphoreType.DMA((11,)),
+        ],
+        compiler_params=pltpu.CompilerParams(vmem_limit_bytes=56 << 20),
         name="write",
     )(feat, w_in, b_in, w_out)
 
 
 def on_device(points, w_in, b_in, w_out, inv_scale, solves, probes):
     vmem = pl.BlockSpec(memory_space=pltpu.VMEM)
-    hbm = pl.BlockSpec(memory_space=pl.ANY)
+    hbm = pl.BlockSpec(memory_space=pltpu.HBM)
+    free = pl.BlockSpec(memory_space=pl.ANY)
     parts = pl.pallas_call(
         kernel,
         out_shape=(
@@ -459,7 +473,7 @@
             jax.ShapeDtypeStruct((FEAT, HID), F32),
         ),
         in_specs=[hbm, hbm, vmem, vmem, vmem, hbm, hbm],
-        out_specs=(vmem, hbm, vmem, vmem),
+        out_specs=(vmem, free, vmem, vmem),
         scratch_shapes=[
             pltpu.VMEM((TOK, DIN), BF16),
             pltpu.VMEM((DIN, HID), BF16),
@@ -481,14 +495,14 @@
             pltpu.VMEM((2, FEAT, HALF), BF16),
             pltpu.VMEM((FEAT, TOK), BF16),
             pltpu.VMEM((2, ROWS, HID), BF16),
-            pltpu.VMEM((7, ROWS, 128), BF16),
+            pltpu.VMEM((8, ROWS, 128), BF16),
             pltpu.VMEM((NZ, 32, 128), BF16),
             pltpu.VMEM((7, 32, 128), BF16),
             pltpu.VMEM((ROWS, 128), BF16),
             pltpu.VMEM((2, 2, 2, ROWS, HID), BF16),
             pltpu.SemaphoreType.DMA((7,)),
-            pltpu.SemaphoreType.DMA((87,)),
-            pltpu.SemaphoreType.DMA((87,)),
+            pltpu.SemaphoreType.DMA((95,)),
+            pltpu.SemaphoreType.DMA((95,)),
             pltpu.SemaphoreType.DMA((8,)),
         ],
         compiler_params=pltpu.CompilerParams(

time: 81 us -> 85 us (1.049)
  Pallas kernels: 80.1 us -> 84.1 us
    pallas_call x1, Pallas kernels: 3.73 us -> 7.31 us  [write(): pl.pallas_call(write_kernel, out_shape=tuple((jax.ShapeDtypeStruct(part.s...]
where the time goes in v6:
time: 85 us; the launch traced here: 84.9 us
  Pallas kernels  84.1 us (99%)
    pallas_call x1, Pallas kernels, on_device(): pl.pallas_call(kernel, out_shape=(jax.ShapeDtypeStruct((FEAT, QUARTER), F...  76.8 us
    pallas_call x1, Pallas kernels, write(): pl.pallas_call(write_kernel, out_shape=tuple((jax.ShapeDtypeStruct(part.s...  7.31 us

profile of v6, /device:TPU:1, one launch (start us, length us, event | category | flops | bytes accessed | tf_op | source)
XLA Modules:
  0.0 84.9 jit_solution(11854809413610817750)
XLA Ops:
  0.6 76.8 %trace_term.1 = (f32[64,192]{1,0:T(8,128)}, bf16[1024,512]{1,0:T(8,128)(2,1)}, f32[1,512]{1,0:T(1,128)}, f32[64,512]{1,0:T(8,128)}) custom-call(bf16[768,1024]{1,0:T(8,128)(2,1)} %points_in.1, bf16[1024,512]{1,0:T(8,128)(2,1)} %w_in_any.1, f32[1,512]{1,0:T(1,128)} %bitcast.6, bf16[64,512]{1,0:T(8,128)(2,1)} %bitcast.5, f32[1,64]{1,0:T(1,128)} %bitcast.7, ...), custom_call_target="tpu_custom_call" | custom-call | tf_op jit(solution)/shard_map/trace_term/pallas_call | solution.py:467
  77.4 7.3 %write.1 = (f32[64,192]{1,0:T(8,128)}, f32[1024,512]{1,0:T(8,128)}, f32[1,512]{1,0:T(1,128)}, f32[64,512]{1,0:T(8,128)}) custom-call(f32[64,192]{1,0:T(8,128)} %get-tuple-element.12.feat, bf16[1024,512]{1,0:T(8,128)(2,1)} %get-tuple-element.13.w_in, f32[1,512]{1,0:T(1,128)} %get-tuple-element.14.b_in, f32[64,512]{1,0:T(8,128)} %get-tuple-element.15.w_out), custom_call_target="tpu_custom_call" | custom-call | tf_op jit(solution)/shard_map/write/pallas_call | solution.py:447

commit v7 on v5

--- a/solution.py
+++ b/solution.py
@@ -77,6 +77,7 @@
     near = [device(one, z, y_lo, y_hi, c) for one in (x_next, x_prev, x_far)]
     near += [device(x, one, y_lo, y_hi, c) for one in (z_next, z_prev)]
     near += [device(x, one, 1 - y_lo, y_hi, c) for one in (z, z_next, z_prev)]
+    near += [device(x, one, 1 - y_lo, 1 - y_hi, c) for one in (z, z_next, z_prev)]
     near += [twin, device(x, z, y_lo, 1 - y_hi, c)]
 
     def lanes(index):
@@ -141,7 +142,40 @@
         return copy(n, own.at[pieces[n]], vis.at[1, pieces[n]], visited)
 
     def to_base(n):
-        return copy(3 + n, own.at[pieces[n], side], vis.at[0, pieces[n], side], device(x, z, 1 - y_lo, y_hi, c))
+        return copy(3 + n, own.at[pieces[n], side], vis.at[0, pieces[n], side], device(x, z, 1 - y_lo, 1, c))
+
+    def to_cross(n):
+        return copy(95 + n, own.at[pieces[n]], vis.at[1, pieces[n]], device(x, z_next, 1 - y_lo, 1, c))
+
+    gives_base = (y_hi + c) == 1
+    keeps_chain = (y_hi == 0) | (c == 0)
+    gives_cross = (y_hi == 0) & (c == 1)
+    takes_cross = (y_hi == 1) & (c == 1)
+
+    def first_sends(which):
+        @pl.when(gives_base)
+        def _():
+            for n in which:
+                to_base(n).start()
+
+        @pl.when(keeps_chain)
+        def _():
+            for n in which:
+                to_vis(n).start()
+
+        @pl.when(gives_cross)
+        def _():
+            for n in which:
+                to_cross(n).start()
+
+    def first_arrived(n):
+        @pl.when(keeps_chain)
+        def _():
+            to_vis(n).wait_recv()
+
+        @pl.when(takes_cross)
+        def _():
+            to_cross(n).wait_recv()
 
     def share_base(n):
         part = vis.at[0, pieces[n], side]
@@ -162,7 +196,10 @@
 
     def pump(hop, which):
         for n in which:
-            (to_vis(n) if hop == 1 else to_z(hop - 1, n)).wait_recv()
+            if hop == 1:
+                first_arrived(n)
+            else:
+                to_z(hop - 1, n).wait_recv()
             if hop < 4:
                 started.append(to_z(hop, n))
                 started[-1].start()
@@ -176,14 +213,7 @@
             half_own[rows, q * QUARTER : (q + 1) * QUARTER] = picked
         held[rows, lanes(x)] = half_own[rows, :]
 
-    @pl.when(y_hi == 1)
-    def _():
-        for n in vectors:
-            to_base(n).start()
-
-    for n in vectors:
-        started.append(to_vis(n))
-        started[-1].start()
+    first_sends(vectors)
     keep_half(pairs)
     pair_x = {}
     feat_x = {}
@@ -206,12 +236,7 @@
     scale = jnp.sum(jnp.where(eye, scale_row_v, 0.0), axis=1, keepdims=True)
     scaled = (dot(w_t[...], hidden[...], 1, 1) * scale).astype(BF16)
     own[feats, :] = scaled
-    @pl.when(y_hi == 1)
-    def _():
-        to_base(2).start()
-
-    started.append(to_vis(2))
-    started[-1].start()
+    first_sends((2,))
     keep_half(feats)
     send_feat(1)
     send_feat(3)
@@ -355,8 +380,10 @@
         summed = summed + recv_a[d - 1].astype(F32)
     summed_b = summed.astype(BF16)
     for b in range(NZ):
+        far = (b + 4) % NZ
         stage_b[b, 0:16, :] = summed_b[b * 16 : b * 16 + 16]
-        stage_b[b, 16:32, :] = summed_b[128:144]
+        stage_b[b, 16:32, :] = summed_b[far * 16 : far * 16 + 16]
+        stage_b[b, 32:48, :] = summed_b[128:144]
     arrivals = []
     for d in (4, 3, 5, 2, 6, 1, 7):
         pz = column[d - 1]
@@ -367,13 +394,15 @@
     for d in range(1, 8):
         tile = tile + recv_b[d - 1].astype(F32)
     tile_b = tile.astype(BF16)
-    band = aligned(z * 16, 16, 16)
-    chunk[band, :] = tile_b[0:16]
-    chunk[128:144, :] = tile_b[16:32]
+    bands = [aligned(z * 16, 16, 16), aligned(lax.rem(z + 4, NZ) * 16, 16, 16)]
+    chunk[bands[0], :] = tile_b[0:16]
+    chunk[bands[1], :] = tile_b[16:32]
+    chunk[128:144, :] = tile_b[32:48]
     arrivals = []
-    for d in (4, 3, 5, 2, 6, 1, 7):
-        pz = column[d - 1]
-        arrivals.append(send(58 + d, chunk.at[band], chunk.at[band], device(x, pz, y_lo, y_hi, c)))
+    for n, d in enumerate((6, 1, 7)):
+        for m, band in enumerate(bands):
+            peer = device(x, column[d - 1], y_lo, y_hi, c)
+            arrivals.append(send(59 + 2 * n + m, chunk.at[band], chunk.at[band], peer))
     for one in arrivals:
         one.wait_recv()
     place_mine = table.at[y_hi, c, y_lo, :, strip(x)]
@@ -419,30 +448,57 @@
     @pl.when(y_hi == 1)
     def _():
         for n in everything:
+            share_base(n).wait_send()
+
+    @pl.when(gives_base)
+    def _():
+        for n in everything:
             to_base(n).wait_send()
-            share_base(n).wait_send()
-
-
-def write_kernel(feat, w_in, b_in, w_out, feat_out, w_in_out, b_in_out, w_out_out):
+
+    @pl.when(keeps_chain)
+    def _():
+        for n in everything:
+            to_vis(n).wait_send()
+
+    @pl.when(gives_cross)
+    def _():
+        for n in everything:
+            to_cross(n).wait_send()
+
+
+def write_kernel(feat, w_in, b_in, w_out, feat_out, w_in_out, b_in_out, w_out_out, narrow, wide, load_sem, store_sem):
+    count = 4
+    rows = [slice(i * DIN // count, (i + 1) * DIN // count) for i in range(count)]
+    loads = [pltpu.make_async_copy(w_in.at[r], narrow.at[r], load_sem.at[i]) for i, r in enumerate(rows)]
+    stores = [pltpu.make_async_copy(wide.at[r], w_in_out.at[r], store_sem.at[i]) for i, r in enumerate(rows)]
+    for one in loads:
+        one.start()
     feat_out[...] = feat[...]
-    w_in_out[...] = w_in[...].astype(F32)
     b_in_out[...] = b_in[...]
     w_out_out[...] = w_out[...]
+    for i, r in enumerate(rows):
+        loads[i].wait()
+        wide[r] = narrow[r].astype(F32)
+        stores[i].start()
+    for one in stores:
+        one.wait()
 
 
 def write(feat, w_in, b_in, w_out):
-    specs = []
-    for part in (feat, w_in, b_in, w_out):
-        if part is w_in:
-            specs.append(pl.BlockSpec((DIN // 4, HID), lambda i: (i, 0)))
-        else:
-            specs.append(pl.BlockSpec(part.shape, lambda i: (0, 0)))
+    free = pl.BlockSpec(memory_space=pltpu.HBM)
+    vmem = pl.BlockSpec(memory_space=pltpu.VMEM)
     return pl.pallas_call(
         write_kernel,
-        grid=(4,),
         out_shape=tuple(jax.ShapeDtypeStruct(part.shape, F32) for part in (feat, w_in, b_in, w_out)),
-        in_specs=specs,
-        out_specs=tuple(specs),
+        in_specs=[vmem, free, vmem, vmem],
+        out_specs=(vmem, free, vmem, vmem),
+        scratch_shapes=[
+            pltpu.VMEM((DIN, HID), BF16),
+            pltpu.VMEM((DIN, HID), F32),
+            pltpu.SemaphoreType.DMA((4,)),
+            pltpu.SemaphoreType.DMA((4,)),
+        ],
+        compiler_params=pltpu.CompilerParams(vmem_limit_bytes=56 << 20),
         name="write",
     )(feat, w_in, b_in, w_out)
 
@@ -482,13 +538,13 @@
             pltpu.VMEM((FEAT, TOK), BF16),
             pltpu.VMEM((2, ROWS, HID), BF16),
             pltpu.VMEM((7, ROWS, 128), BF16),
-            pltpu.VMEM((NZ, 32, 128), BF16),
-            pltpu.VMEM((7, 32, 128), BF16),
+            pltpu.VMEM((NZ, 48, 128), BF16),
+            pltpu.VMEM((7, 48, 128), BF16),
             pltpu.VMEM((ROWS, 128), BF16),
             pltpu.VMEM((2, 2, 2, ROWS, HID), BF16),
             pltpu.SemaphoreType.DMA((7,)),
-            pltpu.SemaphoreType.DMA((87,)),
-            pltpu.SemaphoreType.DMA((87,)),
+            pltpu.SemaphoreType.DMA((98,)),
+            pltpu.SemaphoreType.DMA((98,)),
             pltpu.SemaphoreType.DMA((8,)),
         ],
         compiler_params=pltpu.CompilerParams(

time: 81 us -> 76.2 us (0.941)
  Pallas kernels: 80.1 us -> 75.2 us
    pallas_call x1, Pallas kernels: 76.4 us -> 71.2 us  [on_device(): pl.pallas_call(kernel, out_shape=(jax.ShapeDtypeStruct((FEAT, QUARTER), F...]
where the time goes in v7:
time: 76.2 us; the launch traced here: 76 us
  Pallas kernels  75.2 us (99%)
  between operations  0.8 us (1%)
    pallas_call x1, Pallas kernels, on_device(): pl.pallas_call(kernel, out_shape=(jax.ShapeDtypeStruct((FEAT, QUARTER), F...  71.2 us
    pallas_call x1, Pallas kernels, write(): pl.pallas_call(write_kernel, out_shape=tuple((jax.ShapeDtypeStruct(part.s...  3.99 us

profile of v7, /device:TPU:1, one launch (start us, length us, event | category | flops | bytes accessed | tf_op | source)
XLA Modules:
  0.0 76.0 jit_solution(1348544407700219915)
XLA Ops:
  0.6 71.2 %trace_term.1 = (f32[64,192]{1,0:T(8,128)}, bf16[1024,512]{1,0:T(8,128)(2,1)}, f32[1,512]{1,0:T(1,128)}, f32[64,512]{1,0:T(8,128)}) custom-call(bf16[768,1024]{1,0:T(8,128)(2,1)} %points_in.1, bf16[1024,512]{1,0:T(8,128)(2,1)} %w_in_any.1, f32[1,512]{1,0:T(1,128)} %bitcast.6, bf16[64,512]{1,0:T(8,128)(2,1)} %bitcast.5, f32[1,64]{1,0:T(1,128)} %bitcast.7, ...), custom_call_target="tpu_custom_call" | custom-call | tf_op jit(solution)/shard_map/trace_term/pallas_call | solution.py:509
  71.9 4.0 %write.1 = (f32[64,192]{1,0:T(8,128)}, f32[1024,512]{1,0:T(8,128)}, f32[1,512]{1,0:T(1,128)}, f32[64,512]{1,0:T(8,128)}) custom-call(f32[64,192]{1,0:T(8,128)} %get-tuple-element.12.feat, bf16[1024,512]{1,0:T(8,128)(2,1)} %get-tuple-element.13.w_in, f32[1,512]{1,0:T(1,128)} %get-tuple-element.14.b_in, f32[64,512]{1,0:T(8,128)} %get-tuple-element.15.w_out), custom_call_target="tpu_custom_call" | custom-call | tf_op jit(solution)/shard_map/write/pallas_call | solution.py:490

commit v8 on v7

--- a/solution.py
+++ b/solution.py
@@ -125,8 +125,6 @@
 
     loads[5].wait()
     loads[6].wait()
-    loads[0].wait()
-    features(0)
     pl.semaphore_wait(barrier, len(near))
 
     pairs = slice(FEAT, MSG)
@@ -229,7 +227,8 @@
     send_pair(1)
     send_pair(3)
     send_pair(2)
-    for i in range(1, 4):
+    loads[0].wait()
+    for i in range(4):
         features(i)
     scale_row_v = scale_row[...]
     eye = lax.broadcasted_iota(jnp.int32, (FEAT, FEAT), 0) == lax.broadcasted_iota(jnp.int32, (FEAT, FEAT), 1)
@@ -352,32 +351,33 @@
 
     norm = 1.0 / math.sqrt(NPTS)
     pre = dot(grad[...], w_t[...], 0, 0) * slope[...]
-    gw = dot(slab_t[...], pre.astype(BF16), 1, 0) * norm
-    bias = jnp.sum(pre, axis=0, keepdims=True) * norm
-    gwo = dot(grad[aligned(rep * 16, 16, 16), :], hidden[...], 1, 0) * norm
-    msg[0, 0:128, :] = gw[0:128].astype(BF16)
-    msg[1, 0:128, :] = gw[128:256].astype(BF16)
-    msg[0, 128:144, :] = gwo.astype(BF16)
-    msg[1, 128:144, :] = jnp.broadcast_to(bias, (16, HID)).astype(BF16)
-
+    pre_b = pre.astype(BF16)
     def strip(px):
         return aligned(px * 128, 128, 128)
 
-    cell = y_lo * NX + x
-    plane = []
     column = []
     for d in range(1, 8):
-        other = lax.rem(cell + d, 8)
-        plane.append((lax.rem(other, NX), lax.div(other, NX)))
         column.append(lax.rem(z + d, NZ))
     arrivals = []
-    for d in range(1, 8):
-        px, py = plane[d - 1]
-        arrivals.append(send(44 + d, msg.at[py, :, strip(px)], recv_a.at[d - 1], device(px, z, py, y_hi, c)))
+
+    def scatter(row, first):
+        msg[row, 0:128, :] = (dot(slab_t[aligned(row * 128, 128, 128), :], pre_b, 1, 0) * norm).astype(BF16)
+        small = jnp.where(row == 0, gwo, bias)
+        msg[row, 128:144, :] = small.astype(BF16)
+        for dx in (2, 1, 3) if first is None else (2, 1, 3, 0):
+            px = lax.rem(x + dx, NX)
+            at = (first or 0) + dx
+            arrivals.append(send(45 + at, msg.at[row, :, strip(px)], recv_a.at[at], device(px, z, row, y_hi, c)))
+
+    gwo = dot(grad[aligned(rep * 16, 16, 16), :], hidden[...], 1, 0) * norm
+    bias = jnp.broadcast_to(jnp.sum(pre, axis=0, keepdims=True) * norm, (16, HID))
+    scatter(1 - y_lo, 4)
+    scatter(y_lo, None)
     summed = msg[y_lo, :, strip(x)].astype(F32)
-    for d in range(1, 8):
-        arrivals[d - 1].wait_recv()
-        summed = summed + recv_a[d - 1].astype(F32)
+    for one in arrivals:
+        one.wait_recv()
+    for at in range(1, 8):
+        summed = summed + recv_a[at].astype(F32)
     summed_b = summed.astype(BF16)
     for b in range(NZ):
         far = (b + 4) % NZ
@@ -387,7 +387,7 @@
     arrivals = []
     for d in (4, 3, 5, 2, 6, 1, 7):
         pz = column[d - 1]
-        arrivals.append(send(51 + d, stage_b.at[pz], recv_b.at[d - 1], device(x, pz, y_lo, y_hi, c)))
+        arrivals.append(send(87 + d, stage_b.at[pz], recv_b.at[d - 1], device(x, pz, y_lo, y_hi, c)))
     for one in arrivals:
         one.wait_recv()
     tile = stage_b[z].astype(F32)
@@ -537,7 +537,7 @@
             pltpu.VMEM((2, FEAT, HALF), BF16),
             pltpu.VMEM((FEAT, TOK), BF16),
             pltpu.VMEM((2, ROWS, HID), BF16),
-            pltpu.VMEM((7, ROWS, 128), BF16),
+            pltpu.VMEM((8, ROWS, 128), BF16),
             pltpu.VMEM((NZ, 48, 128), BF16),
             pltpu.VMEM((7, 48, 128), BF16),
             pltpu.VMEM((ROWS, 128), BF16),

time: 76.2 us -> 75.4 us (0.990)
  Pallas kernels: 75.2 us -> 74.4 us
    pallas_call x1, Pallas kernels: 71.2 us -> 70.4 us  [on_device(): pl.pallas_call(kernel, out_shape=(jax.ShapeDtypeStruct((FEAT, QUARTER), F...]
where the time goes in v8:
time: 75.4 us; the launch traced here: 75.2 us
  Pallas kernels  74.4 us (99%)
  between operations  0.8 us (1%)
    pallas_call x1, Pallas kernels, on_device(): pl.pallas_call(kernel, out_shape=(jax.ShapeDtypeStruct((FEAT, QUARTER), F...  70.4 us
    pallas_call x1, Pallas kernels, write(): pl.pallas_call(write_kernel, out_shape=tuple((jax.ShapeDtypeStruct(part.s...  3.99 us

profile of v8, /device:TPU:1, one launch (start us, length us, event | category | flops | bytes accessed | tf_op | source)
XLA Modules:
  0.0 75.2 jit_solution(8613436995675246255)
XLA Ops:
  0.6 70.4 %trace_term.1 = (f32[64,192]{1,0:T(8,128)}, bf16[1024,512]{1,0:T(8,128)(2,1)}, f32[1,512]{1,0:T(1,128)}, f32[64,512]{1,0:T(8,128)}) custom-call(bf16[768,1024]{1,0:T(8,128)(2,1)} %points_in.1, bf16[1024,512]{1,0:T(8,128)(2,1)} %w_in_any.1, f32[1,512]{1,0:T(1,128)} %bitcast.6, bf16[64,512]{1,0:T(8,128)(2,1)} %bitcast.5, f32[1,64]{1,0:T(1,128)} %bitcast.7, ...), custom_call_target="tpu_custom_call" | custom-call | tf_op jit(solution)/shard_map/trace_term/pallas_call | solution.py:509
  71.1 4.0 %write.1 = (f32[64,192]{1,0:T(8,128)}, f32[1024,512]{1,0:T(8,128)}, f32[1,512]{1,0:T(1,128)}, f32[64,512]{1,0:T(8,128)}) custom-call(f32[64,192]{1,0:T(8,128)} %get-tuple-element.12.feat, bf16[1024,512]{1,0:T(8,128)(2,1)} %get-tuple-element.13.w_in, f32[1,512]{1,0:T(1,128)} %get-tuple-element.14.b_in, f32[64,512]{1,0:T(8,128)} %get-tuple-element.15.w_out), custom_call_target="tpu_custom_call" | custom-call | tf_op jit(solution)/shard_map/write/pallas_call | solution.py:490
